TPU v7x, 512 devices: a whole 4x4x16 slice. The times are simulated.
512 devices in a mesh: dom: 64 (over z, y), sub: 8 (over x, core).
Axes of the slice: x: 4, y: 4, z: 16, core: 2. Of those that a mesh axis runs over, the one named last changes fastest.
Arguments:
- fields: float32 [6, 56, 131072], P(None, None, ('dom', 'sub')), may hold values from -6 to 6
- metric: float32 [9, 131072], P(None, ('dom', 'sub')), may hold values from -4 to 4
- face_geom: float32 [4, 4, 131072], P(None, None, ('dom', 'sub')), as said below
- jacobian_ratio: float32 [56, 131072], P(None, ('dom', 'sub')), may hold values from 0.5 to 2
- curved: int32 [131072], P(('dom', 'sub')), may hold values 0 or 1
- derivatives: float32 [3, 56, 56], replicated, may hold values from -0.75 to 0.75
- lift_matrix: float32 [56, 84], replicated, may hold values from -0.625 to 0.625
- live_count: int32 [512], P(('dom', 'sub')), may hold values from 128 to 256, as said below
- send_list: int32 [512, 3, 8, 32], P(('dom', 'sub')), may hold values from 0 to 1023, as said below
- face_source: int32 [4, 131072], P(None, ('dom', 'sub')), may hold values from 0 to 1791, as said below
- face_permutation: int32 [4, 131072], P(None, ('dom', 'sub')), may hold values from 0 to 5
Outputs:
- advanced: float32 [6, 56, 131072], P(None, None, ('dom', 'sub'))
- section_register: float32 [6, 56, 131072], P(None, None, ('dom', 'sub'))
Inputs may be any that keep to these rules, and one draw needn't show every extreme that they name: `live_count`: some device owns exactly 256 elements. `send_list`: each entry names a face f * 256 + e of an element that its device owns. `face_source`: an entry below 1024 names a face of an owned element of the same device; a larger entry names a ghost slot, never one whose source group lies outside the mesh. `face_geom`: unit normals and a positive surface scale.
All inputs are finite; a program needn't handle non-finite values. No bound on the sum of `curved` on one device may be relied on, other than what follows from the above.
Results may differ from a plain program's by a relative error of at most 0.0003.
Values sent between devices are 32-bit elements; how exact they have to be, the bound alone decides.
No kernel may reach another device: no remote copies, remote signals or barrier semaphores. Data moves between devices by JAX's collectives and lax.ppermute only.
A program may use at most 128 MiB of HBM per device.

v0:
```python
import jax
import jax.numpy as jnp
import numpy as np
from jax import lax
from jax.sharding import PartitionSpec as P

RK_A = (0.0, -567301805773.0 / 1357537059087.0)
RK_B = (1432997174477.0 / 9575080441755.0, 5161836677717.0 / 13612068292357.0)
TIME_STEP = 0.5
SYMMETRIES = ((0, 1, 2), (1, 2, 0), (2, 0, 1), (0, 2, 1), (2, 1, 0), (1, 0, 2))


def passed_along(array, axis, by):
    count = lax.axis_size(axis)
    pairs = [(i, i + by) for i in range(count) if 0 <= i + by < count]
    return lax.ppermute(array, axis, pairs)


def node_tables():
    volume_nodes = [(i, j, k) for i in range(6) for j in range(6 - i) for k in range(6 - i - j)]
    volume_index = {v: n for n, v in enumerate(volume_nodes)}
    triangle = [(a, b) for a in range(6) for b in range(6 - a)]
    triangle_index = {t: n for n, t in enumerate(triangle)}
    face_nodes = np.array(
        [
            [volume_index[a, b, 0] for a, b in triangle],
            [volume_index[a, 0, b] for a, b in triangle],
            [volume_index[a, b, 5 - a - b] for a, b in triangle],
            [volume_index[0, a, b] for a, b in triangle],
        ],
        np.int32,
    )
    permuted = np.array(
        [
            [triangle_index[(a, b, 5 - a - b)[q[0]], (a, b, 5 - a - b)[q[1]]] for a, b in triangle]
            for q in SYMMETRIES
        ],
        np.int32,
    )
    return (face_nodes, permuted)


def volume_and_flux(current, exterior, interior, metric, face_geom, derivatives):
    slopes = jnp.einsum("mpq,cqe->mcpe", derivatives, current, precision=lax.Precision.HIGHEST)
    gradients = [
        metric[x] * slopes[0] + metric[3 + x] * slopes[1] + metric[6 + x] * slopes[2]
        for x in range(3)
    ]
    diff_x, diff_y, diff_z = gradients
    volume = jnp.stack(
        [
            -(diff_y[5] - diff_z[4]),
            -(diff_z[3] - diff_x[5]),
            -(diff_x[4] - diff_y[3]),
            diff_y[2] - diff_z[1],
            diff_z[0] - diff_x[2],
            diff_x[1] - diff_y[0],
        ]
    )
    jump = exterior - interior
    normal_x, normal_y, normal_z, face_scale = (
        face_geom[0],
        face_geom[1],
        face_geom[2],
        face_geom[3],
    )
    along_h = normal_x * jump[0] + normal_y * jump[1] + normal_z * jump[2]
    along_e = normal_x * jump[3] + normal_y * jump[4] + normal_z * jump[5]
    flux_all = jnp.stack(
        [
            -(normal_y * jump[5] - normal_z * jump[4]) + jump[0] - along_h * normal_x,
            -(normal_z * jump[3] - normal_x * jump[5]) + jump[1] - along_h * normal_y,
            -(normal_x * jump[4] - normal_y * jump[3]) + jump[2] - along_h * normal_z,
            normal_y * jump[2] - normal_z * jump[1] + jump[3] - along_e * normal_x,
            normal_z * jump[0] - normal_x * jump[2] + jump[4] - along_e * normal_y,
            normal_x * jump[1] - normal_y * jump[0] + jump[5] - along_e * normal_z,
        ]
    ) * (0.5 * face_scale)
    return (volume, flux_all)


def on_device(
    fields,
    metric,
    face_geom,
    jacobian_ratio,
    curved,
    derivatives,
    lift_matrix,
    live_count,
    send_list,
    face_source,
    face_permutation,
):
    face_nodes, permuted = node_tables()
    elements = fields.shape[2]
    node_count = fields.shape[1]
    trace_nodes = face_nodes.shape[1]
    alive_mask = (jnp.arange(elements, dtype=jnp.int32) < live_count[0]).astype(jnp.float32)
    scaling = jnp.where(curved == 1, jacobian_ratio, 1.0) * alive_mask
    outgoing_index = send_list.reshape(-1)
    turn_rows = jnp.transpose(jnp.asarray(permuted)[face_permutation], (2, 0, 1))
    lift_three = lift_matrix.reshape(node_count, 4, trace_nodes)
    current = fields * alive_mask
    residual = jnp.zeros_like(fields)
    for step_index in range(2):
        interior = current[:, face_nodes.T, :]
        table_local = interior.reshape(6, trace_nodes, 4 * elements)
        outgoing = jnp.take(table_local, outgoing_index, axis=2).reshape(
            (6, trace_nodes) + send_list.shape[1:]
        )
        swapped = lax.all_to_all(outgoing, "sub", split_axis=3, concat_axis=3, tiled=True)
        upward = passed_along(swapped[:, :, 2], "dom", 1)
        downward = passed_along(swapped[:, :, 0], "dom", -1)
        received = jnp.stack([downward, swapped[:, :, 1], upward], axis=2)
        table = jnp.concatenate([table_local, received.reshape(6, trace_nodes, -1)], axis=2)
        columns = table.shape[2]
        flat_index = (turn_rows * columns + face_source[None]).reshape(-1)
        exterior = jnp.take(table.reshape(6, -1), flat_index, axis=1).reshape(
            6, trace_nodes, 4, elements
        )
        volume, flux_all = volume_and_flux(
            current, exterior, interior, metric, face_geom, derivatives
        )
        lifted = jnp.einsum("nfi,cife->cne", lift_three, flux_all, precision=lax.Precision.HIGHEST)
        rate = (volume + lifted) * scaling
        residual = RK_A[step_index] * residual + TIME_STEP * rate
        current = current + RK_B[step_index] * residual
    return (current, residual)


def solution(mesh):
    return jax.shard_map(
        on_device,
        mesh=mesh,
        in_specs=(
            P(None, None, ("dom", "sub")),
            P(None, ("dom", "sub")),
            P(None, None, ("dom", "sub")),
            P(None, ("dom", "sub")),
            P(("dom", "sub")),
            P(),
            P(),
            P(("dom", "sub")),
            P(("dom", "sub"), None, None, None),
            P(None, ("dom", "sub")),
            P(None, ("dom", "sub")),
        ),
        out_specs=(P(None, None, ("dom", "sub")), P(None, None, ("dom", "sub"))),
        check_vma=False,
    )
```

profile of v0, /device:TPU:384, one launch (start us, length us, event | category | flops | bytes accessed | tf_op | source)
XLA Modules:
  0.0 346.0 jit_solution(4009709944031995420)
XLA Ops:
  0.6 0.8 reshape.83
  2.1 0.7 compare_convert_fusion
  2.8 1.0 broadcast_multiply_fusion.3
  3.8 0.7 copy-done.5
  4.7 0.7 pad_clamp_fusion
  5.3 0.7 gather_fusion
  7.1 2.7 copy.57
  9.8 5.0 %gather_fusion.3 = f32[768,6,21]{2,1,0:T(8,128)} fusion(f32[6,21,1024]{1,0,2:T(8,128)} %copy.57, s32[1024]{0:T(1024)S(1)} %get-tuple-element.43), kind=kCustom, calls=%fused_computation.clone | custom fusion | bytes 777216 | tf_op jit(solution)/shard_map/jit(_take)/gather | solution.py:109
  14.9 4.4 %broadcast_select_fusion.3 = f32[768,6,21]{2,1,0:T(8,128)S(1)} fusion(f32[768,6,21]{2,1,0:T(8,128)} %gather_fusion.3, pred[768]{0:T(1024)(128)(4,1)S(1)} %compare_and_fusion.1), kind=kLoop, calls=%fused_computation.10 | loop fusion | flops 96768 | bytes 774912 | tf_op jit(solution)/shard_map/jit(_take)/select_n | solution.py:109
  19.3 2.2 copy.58
  21.4 3.0 reshape.176
  24.4 4.3 %all-to-all-start = ((f32[8,1,12096]{2,1,0:T(1,128)}), f32[8,1,12096]{2,1,0:T(1,128)S(1)}, u32[]{:S(2)}, u32[]{:S(2)}) async-start(f32[8,1,12096]{2,1,0:T(1,128)} %reshape.176), calls=%async_computation | async-start | bytes 778240 | tf_op jit(solution)/shard_map/all_to_all | solution.py:112
  28.8 2.8 gather_fusion.1
  32.1 1.0 convolution_bitcast_fusion.1
  33.5 4.1 %all-to-all-done = f32[8,1,12096]{2,1,0:T(1,128)S(1)} async-done(((f32[8,1,12096]{2,1,0:T(1,128)}), f32[8,1,12096]{2,1,0:T(1,128)S(1)}, u32[]{:S(2)}, u32[]{:S(2)}) %all-to-all-start) | async-done | bytes 387104 | tf_op jit(solution)/shard_map/all_to_all | solution.py:112
  38.2 1.5 reduce
  39.7 0.7 reshape.177
  40.7 6.6 %collective-permute-start = (f32[6,21,8,32]{3,2,1,0:T(8,128)S(1)}, f32[6,21,8,32]{3,2,1,0:T(8,128)S(1)}, u32[]{:S(2)}, u32[]{:S(2)}) collective-permute-start(f32[6,21,8,32]{3,2,1,0:T(8,128)S(1)} %copy.59), channel_id=1, source_target_pairs={{8,0},{16,8},{24,16},{32,24},{40,32},{48,40},{56,48},{64,56},{72,6... | collective-permute-start | bytes 387080 | tf_op jit(solution)/shard_map/ppermute | solution.py:16
  47.5 2.2 collective-permute-start.1
  49.9 8.2 %collective-permute-done = f32[6,21,8,32]{3,2,1,0:T(8,128)S(1)} collective-permute-done((f32[6,21,8,32]{3,2,1,0:T(8,128)S(1)}, f32[6,21,8,32]{3,2,1,0:T(8,128)S(1)}, u32[]{:S(2)}, u32[]{:S(2)}) %collective-permute-start) | collective-permute-done | bytes 129056 | tf_op jit(solution)/shard_map/ppermute | solution.py:16
  58.1 7.8 %collective-permute-done.1 = f32[6,21,8,32]{3,2,1,0:T(8,128)S(1)} collective-permute-done((f32[6,21,8,32]{3,2,1,0:T(8,128)S(1)}, f32[6,21,8,32]{3,2,1,0:T(8,128)S(1)}, u32[]{:S(2)}, u32[]{:S(2)}) %collective-permute-start.1) | collective-permute-done | bytes 129056 | tf_op jit(solution)/shard_map/ppermute | solution.py:16
  66.6 9.6 %copy.64 = f32[6,21,1792]{0,2,1:T(8,128)} copy(f32[6,21,1792]{2,1,0:T(8,128)S(1)} %pad_maximum_fusion.2) | data formatting | bytes 1806336 | tf_op jit(solution)/shard_map/concatenate | solution.py:116
  76.2 78.2 %gather_fusion.4 = f32[21504,6]{1,0:T(8,128)} fusion(f32[6,37632]{0,1:T(8,128)} %bitcast.183, s32[21504]{0:T(1024)S(1)} %fusion.12), kind=kCustom, calls=%fused_computation.1.clone | custom fusion | bytes 1118208 | tf_op jit(solution)/shard_map/jit(_take)/gather | solution.py:119
  154.4 13.1 %broadcast_select_fusion.1 = f32[21504,6]{1,0:T(8,128)} fusion(f32[21504,6]{1,0:T(8,128)} %gather_fusion.4, pred[21504]{0:T(1024)(128)(4,1)S(1)} %compare_and_fusion), kind=kLoop, calls=%fused_computation.8 | loop fusion | flops 129024 | bytes 1053696 | tf_op jit(solution)/shard_map/jit(_take)/select_n | solution.py:119
  167.6 7.0 %copy.65 = f32[6,21,4,256]{3,2,1,0:T(4,128)S(1)} copy(f32[6,21,4,256]{0,3,2,1:T(8,128)} %bitcast.181) | data formatting | bytes 1032192 | tf_op jit(solution)/shard_map/reshape | solution.py:119
  175.6 1.4 multiply_add_fusion.4
  177.7 2.0 convolution_bitcast_fusion
  179.7 0.7 gather_fusion.2
  181.5 2.7 copy.71
  184.3 5.0 %gather_fusion.5 = f32[768,6,21]{2,1,0:T(8,128)} fusion(f32[6,21,1024]{1,0,2:T(8,128)} %copy.71, s32[1024]{0:T(1024)S(1)} %get-tuple-element.43), kind=kCustom, calls=%fused_computation.2.clone | custom fusion | bytes 777216 | tf_op jit(solution)/shard_map/jit(_take)/gather | solution.py:109
  189.3 4.4 %broadcast_select_fusion.2 = f32[768,6,21]{2,1,0:T(8,128)S(1)} fusion(f32[768,6,21]{2,1,0:T(8,128)} %gather_fusion.5, pred[768]{0:T(1024)(128)(4,1)S(1)} %compare_and_fusion.1), kind=kLoop, calls=%fused_computation.9 | loop fusion | flops 96768 | bytes 774912 | tf_op jit(solution)/shard_map/jit(_take)/select_n | solution.py:109
  193.7 2.2 copy.72
  195.8 3.1 reshape.178
  198.9 3.5 all-to-all-start.1
  202.7 0.7 copy-done.17
  203.4 7.8 %all-to-all-done.1 = f32[8,1,12096]{2,1,0:T(1,128)S(1)} async-done(((f32[8,1,12096]{2,1,0:T(1,128)}), f32[8,1,12096]{2,1,0:T(1,128)S(1)}, u32[]{:S(2)}, u32[]{:S(2)}) %all-to-all-start.1) | async-done | bytes 387104 | tf_op jit(solution)/shard_map/all_to_all | solution.py:112
  211.2 1.5 reduce.1
  212.7 0.7 reshape.179
  213.8 1.9 collective-permute-start.2
  215.9 4.3 %collective-permute-start.3 = (f32[6,21,8,32]{3,2,1,0:T(8,128)S(1)}, f32[6,21,8,32]{3,2,1,0:T(8,128)S(1)}, u32[]{:S(2)}, u32[]{:S(2)}) collective-permute-start(f32[6,21,8,32]{3,2,1,0:T(8,128)S(1)} %copy.74), channel_id=1, source_target_pairs={{0,8},{8,16},{16,24},{24,32},{32,40},{40,48},{48,56},{56,64},{64,7... | collective-permute-start | bytes 387080 | tf_op jit(solution)/shard_map/ppermute | solution.py:16
  220.2 0.6 fusion.13
  221.0 8.0 %collective-permute-done.2 = f32[6,21,8,32]{3,2,1,0:T(8,128)S(1)} collective-permute-done((f32[6,21,8,32]{3,2,1,0:T(8,128)S(1)}, f32[6,21,8,32]{3,2,1,0:T(8,128)S(1)}, u32[]{:S(2)}, u32[]{:S(2)}) %collective-permute-start.2) | collective-permute-done | bytes 129056 | tf_op jit(solution)/shard_map/ppermute | solution.py:16
  229.0 5.6 %collective-permute-done.3 = f32[6,21,8,32]{3,2,1,0:T(8,128)S(1)} collective-permute-done((f32[6,21,8,32]{3,2,1,0:T(8,128)S(1)}, f32[6,21,8,32]{3,2,1,0:T(8,128)S(1)}, u32[]{:S(2)}, u32[]{:S(2)}) %collective-permute-start.3) | collective-permute-done | bytes 129056 | tf_op jit(solution)/shard_map/ppermute | solution.py:16
  235.3 9.6 %copy.78 = f32[6,21,1792]{0,2,1:T(8,128)} copy(f32[6,21,1792]{2,1,0:T(8,128)S(1)} %pad_maximum_fusion.3) | data formatting | bytes 1806336 | tf_op jit(solution)/shard_map/concatenate | solution.py:116
  244.9 78.2 %gather_fusion.6 = f32[21504,6]{1,0:T(8,128)} fusion(f32[6,37632]{0,1:T(8,128)} %bitcast.182, s32[21504]{0:T(1024)S(1)} %fusion.12), kind=kCustom, calls=%fused_computation.3.clone | custom fusion | bytes 1118208 | tf_op jit(solution)/shard_map/jit(_take)/gather | solution.py:119
  323.1 13.1 %broadcast_select_fusion = f32[21504,6]{1,0:T(8,128)} fusion(f32[21504,6]{1,0:T(8,128)} %gather_fusion.6, pred[21504]{0:T(1024)(128)(4,1)S(1)} %compare_and_fusion), kind=kLoop, calls=%fused_computation.7 | loop fusion | flops 129024 | bytes 1053696 | tf_op jit(solution)/shard_map/jit(_take)/select_n | solution.py:119
  336.2 7.0 %copy.79 = f32[6,21,4,256]{3,2,1,0:T(4,128)S(1)} copy(f32[6,21,4,256]{0,3,2,1:T(8,128)} %bitcast.180) | data formatting | bytes 1032192 | tf_op jit(solution)/shard_map/reshape | solution.py:119
  344.4 1.6 multiply_add_fusion
  (118 shorter events, 9.4 us)
Async XLA Ops:
  0.6 31.5 %copy-start = (f32[3,56,56]{2,1,0:T(8,128)S(1)}, f32[3,56,56]{2,1,0:T(8,128)}, u32[]{:S(2)}) copy-start(f32[3,56,56]{2,1,0:T(8,128)} %param.25) | copy-start | bytes 112900
  3.8 0.7 copy-start.5
  6.0 0.8 copy-start.11
  7.1 2.7 copy-start.7
  19.3 9.5 %copy-start.26 = (s32[4,256]{1,0:T(4,128)S(1)}, s32[4,256]{1,0:T(4,128)}, u32[]{:S(2)}) copy-start(s32[4,256]{1,0:T(4,128)} %param.30) | copy-start | bytes 12292
  19.3 9.5 %copy-start.2 = (s32[6,21]{1,0:T(8,128)S(1)}, s32[6,21]{1,0:T(8,128)}, u32[]{:S(2)}) copy-start(s32[6,21]{1,0:T(8,128)} %constant.26.clone) | copy-start | bytes 1516
  24.4 13.2 %all-to-all-start = ((f32[8,1,12096]{2,1,0:T(1,128)}), f32[8,1,12096]{2,1,0:T(1,128)S(1)}, u32[]{:S(2)}, u32[]{:S(2)}) async-start(f32[8,1,12096]{2,1,0:T(1,128)} %reshape.176), calls=%async_computation | async-start | bytes 778240 | tf_op jit(solution)/shard_map/all_to_all | solution.py:112
  28.8 3.1 copy-start.25
  28.8 3.3 copy-start.24
  28.8 3.3 copy-start.6
  31.7 1.7 copy-start.21
  31.7 1.7 copy-start.22
  33.5 4.1 %copy-start.19 = (f32[6,56,256]{2,1,0:T(8,128)}, f32[6,56,256]{2,1,0:T(8,128)S(1)}, u32[]{:S(2)}) copy-start(f32[6,56,256]{2,1,0:T(8,128)S(1)} %fusion.22) | copy-start | bytes 1032196
  40.4 9.3 %copy-start.23 = (f32[4,4,256]{2,1,0:T(4,128)S(1)}, f32[4,4,256]{2,1,0:T(4,128)}, u32[]{:S(2)}) copy-start(f32[4,4,256]{2,1,0:T(4,128)} %param.22) | copy-start | bytes 49156
  40.7 17.4 %collective-permute-start = (f32[6,21,8,32]{3,2,1,0:T(8,128)S(1)}, f32[6,21,8,32]{3,2,1,0:T(8,128)S(1)}, u32[]{:S(2)}, u32[]{:S(2)}) collective-permute-start(f32[6,21,8,32]{3,2,1,0:T(8,128)S(1)} %copy.59), channel_id=1, source_target_pairs={{8,0},{16,8},{24,16},{32,24},{40,32},{48,40},{56,48},{64,56},{72,6... | collective-permute-start | bytes 387080 | tf_op jit(solution)/shard_map/ppermute | solution.py:16
  47.5 19.0 %copy-start.8 = (f32[6,21,1024]{2,1,0:T(8,128)S(1)}, f32[6,21,1024]{2,1,0:T(8,128)}, u32[]{:S(2)}) copy-start(f32[6,21,1024]{2,1,0:T(8,128)} %copy-done.7) | copy-start | bytes 1548292
  47.5 18.4 %collective-permute-start.1 = (f32[6,21,8,32]{3,2,1,0:T(8,128)S(1)}, f32[6,21,8,32]{3,2,1,0:T(8,128)S(1)}, u32[]{:S(2)}, u32[]{:S(2)}) collective-permute-start(f32[6,21,8,32]{3,2,1,0:T(8,128)S(1)} %copy.60), channel_id=1, source_target_pairs={{0,8},{8,16},{16,24},{24,32},{32,40},{40,48},{48,56},{56,64},{64,7... | collective-permute-start | bytes 387080 | tf_op jit(solution)/shard_map/ppermute | solution.py:16
  167.6 7.0 %copy-start.12 = (f32[84,6,256]{2,1,0:T(8,128)S(1)}, f32[84,6,256]{2,1,0:T(8,128)}, u32[]{:S(2)}) copy-start(f32[84,6,256]{2,1,0:T(8,128)} %copy-done.11) | copy-start | bytes 1548292
  174.6 1.0 copy-start.20
  177.0 0.7 copy-start.3
  180.4 0.8 copy-start.13
  181.5 2.7 copy-start.9
  195.8 6.6 %copy-start.15 = (f32[3,6,56,256]{3,2,1,0:T(8,128)S(1)}, f32[3,6,56,256]{3,2,1,0:T(8,128)}, u32[]{:S(2)}) copy-start(f32[3,6,56,256]{3,2,1,0:T(8,128)} %convolution_bitcast_fusion) | copy-start | bytes 3096580
  198.9 12.3 %all-to-all-start.1 = ((f32[8,1,12096]{2,1,0:T(1,128)}), f32[8,1,12096]{2,1,0:T(1,128)S(1)}, u32[]{:S(2)}, u32[]{:S(2)}) async-start(f32[8,1,12096]{2,1,0:T(1,128)} %reshape.178), calls=%async_computation.1 | async-start | bytes 778240 | tf_op jit(solution)/shard_map/all_to_all | solution.py:112
  202.7 0.8 copy-start.17
  213.8 15.2 %collective-permute-start.2 = (f32[6,21,8,32]{3,2,1,0:T(8,128)S(1)}, f32[6,21,8,32]{3,2,1,0:T(8,128)S(1)}, u32[]{:S(2)}, u32[]{:S(2)}) collective-permute-start(f32[6,21,8,32]{3,2,1,0:T(8,128)S(1)} %copy.73), channel_id=1, source_target_pairs={{8,0},{16,8},{24,16},{32,24},{40,32},{48,40},{56,48},{64,56},{72,6... | collective-permute-start | bytes 387080 | tf_op jit(solution)/shard_map/ppermute | solution.py:16
  215.9 19.3 %copy-start.10 = (f32[6,21,1024]{2,1,0:T(8,128)S(1)}, f32[6,21,1024]{2,1,0:T(8,128)}, u32[]{:S(2)}) copy-start(f32[6,21,1024]{2,1,0:T(8,128)} %copy-done.9) | copy-start | bytes 1548292
  215.9 18.6 %collective-permute-start.3 = (f32[6,21,8,32]{3,2,1,0:T(8,128)S(1)}, f32[6,21,8,32]{3,2,1,0:T(8,128)S(1)}, u32[]{:S(2)}, u32[]{:S(2)}) collective-permute-start(f32[6,21,8,32]{3,2,1,0:T(8,128)S(1)} %copy.74), channel_id=1, source_target_pairs={{0,8},{8,16},{16,24},{24,32},{32,40},{40,48},{48,56},{56,64},{64,7... | collective-permute-start | bytes 387080 | tf_op jit(solution)/shard_map/ppermute | solution.py:16
  336.2 7.0 %copy-start.14 = (f32[84,6,256]{2,1,0:T(8,128)S(1)}, f32[84,6,256]{2,1,0:T(8,128)}, u32[]{:S(2)}) copy-start(f32[84,6,256]{2,1,0:T(8,128)} %copy-done.13) | copy-start | bytes 1548292
  343.3 1.0 copy-start.4
  343.3 1.1 copy-start.16
  343.3 1.2 copy-start.18
  343.3 2.7 copy-start.1
where the time goes:
time: 347 us; the launch traced here: 346 us
  local copies, waits for them, and re-layouts  230 us (66%)
  other arithmetic  43.6 us (13%)
  waiting for transfers between devices  41.4 us (12%)
  starting transfers between devices  22.8 us (7%)
  matrix products  5.95 us (2%)
    gather x2, local copies, waits for them, and re-layouts, on_device(): jnp.take(table.reshape(6, -1), flat_index, axis=1)  156 us
    ppermute x4, waiting for transfers between devices, passed_along(): return lax.ppermute(array, axis, pairs)  29.5 us
    select_n x2, other arithmetic, on_device(): jnp.take(table.reshape(6, -1), flat_index, axis=1)  26.2 us
    concatenate x2, local copies, waits for them, and re-layouts, on_device(): jnp.concatenate([table_local, received.reshape(6, trace_nodes, -1)], axis=2)  19.2 us
    ppermute x4, starting transfers between devices, passed_along(): return lax.ppermute(array, axis, pairs)  15 us
    reshape x2, local copies, waits for them, and re-layouts, on_device(): jnp.take(table.reshape(6, -1), flat_index, axis=1)  14 us
    all_to_all x2, waiting for transfers between devices, on_device(): lax.all_to_all(outgoing, 'sub', split_axis=3, concat_axis=3, tiled=True)  11.9 us
    unnamed x61, local copies, waits for them, and re-layouts  11.6 us
  transfers between devices with their start and end apart: 6, of which 6 were waited for; matrix products, arithmetic and copies ran while one was open for 2% of the time, Pallas kernels for 0%

commit v1 on v0

v1 whole, which is shorter than its diff:
```python
import functools

import jax
import jax.numpy as jnp
import ml_dtypes
import numpy as np
from jax import lax
from jax.experimental import pallas as pl
from jax.experimental.pallas import tpu as pltpu
from jax.sharding import PartitionSpec as P

RK_A = (0.0, -567301805773.0 / 1357537059087.0)
RK_B = (1432997174477.0 / 9575080441755.0, 5161836677717.0 / 13612068292357.0)
TIME_STEP = 0.5
SYMMETRIES = ((0, 1, 2), (1, 2, 0), (2, 0, 1), (0, 2, 1), (2, 1, 0), (1, 0, 2))

NODES = 56
TRACE = 21
PADDED = 24
PACKED = 128
EXT = 6 * PADDED
F32 = jnp.float32
BF16 = jnp.bfloat16


def passed_along(array, axis, by):
    count = lax.axis_size(axis)
    pairs = [(i, i + by) for i in range(count) if 0 <= i + by < count]
    return lax.ppermute(array, axis, pairs)


def node_tables():
    volume_nodes = [(i, j, k) for i in range(6) for j in range(6 - i) for k in range(6 - i - j)]
    volume_index = {v: n for n, v in enumerate(volume_nodes)}
    triangle = [(a, b) for a in range(6) for b in range(6 - a)]
    triangle_index = {t: n for n, t in enumerate(triangle)}
    face_nodes = np.array(
        [
            [volume_index[a, b, 0] for a, b in triangle],
            [volume_index[a, 0, b] for a, b in triangle],
            [volume_index[a, b, 5 - a - b] for a, b in triangle],
            [volume_index[0, a, b] for a, b in triangle],
        ],
        np.int32,
    )
    permuted = np.array(
        [
            [triangle_index[(a, b, 5 - a - b)[q[0]], (a, b, 5 - a - b)[q[1]]] for a, b in triangle]
            for q in SYMMETRIES
        ],
        np.int32,
    )
    return (face_nodes, permuted)


def constant_matrices():
    face_nodes, permuted = node_tables()
    pick = np.zeros((4 * PACKED, 6 * NODES), np.float32)
    turn = np.zeros((6 * EXT, 2 * PACKED), np.float32)
    for c in range(6):
        for m in range(TRACE):
            for f in range(4):
                pick[f * PACKED + c * TRACE + m, c * NODES + face_nodes[f, m]] = 1
            for p in range(6):
                for part in range(2):
                    turn[p * EXT + c * PADDED + m, part * PACKED + c * TRACE + permuted[p, m]] = 1
    spread_lift = np.zeros((2, 4 * TRACE, 8 * PADDED), np.float32)
    for f in range(4):
        for m in range(TRACE):
            spread_lift[0, f * TRACE + m, f * PADDED + m] = 1
            spread_lift[0, f * TRACE + m, (4 + f) * PADDED + m] = 1
            spread_lift[1, f * TRACE + m, f * PADDED + m] = 1
    spread_node = np.zeros((2, NODES, 2 * NODES), np.float32)
    spread_node[0, :, :NODES] = spread_node[0, :, NODES:] = np.eye(NODES)
    spread_node[1, :, :NODES] = np.eye(NODES)
    return [a.astype(ml_dtypes.bfloat16) for a in (pick, turn, spread_lift, spread_node)]


def mm(a, b):
    return jnp.dot(a, b, preferred_element_type=F32)


def halves(x):
    high = x.astype(BF16)
    return high, (x - high.astype(F32)).astype(BF16)


def stacked_weights(weights, spread):
    high, low = halves(weights)
    return jnp.concatenate([mm(high, spread[0]), mm(low, spread[1])], axis=0).astype(BF16)


def stacked_values(x):
    high = x.astype(BF16).astype(F32)
    return jnp.concatenate([high, x - high], axis=0).astype(BF16)


def split_product(weights, values):
    both = mm(weights, values)
    rows = both.shape[0] // 2
    return both[:rows] + both[rows:]


def traces_of(state, pick):
    high, low = halves(state)
    parts = []
    for part in (high, low):
        all_faces = mm(pick, part).astype(BF16)
        parts.append(
            jnp.concatenate([all_faces[f * PACKED : (f + 1) * PACKED] for f in range(4)], axis=1)
        )
    return jnp.concatenate(parts, axis=0)


def pack(traces, send, out_ref):
    faces = traces.shape[1]
    slots = send.shape[1]
    columns = jnp.transpose(send, (1, 0))
    lane = lax.broadcasted_iota(jnp.int32, (slots, faces), 1)
    for j in range(8):
        rows = []
        for o in range(3):
            r = o * 8 + j
            hit = lane == columns[:, r : r + 1]
            rows.append(jnp.where(hit, 1.0, 0.0).astype(BF16))
        chosen = lax.dot_general(
            jnp.concatenate(rows, axis=0),
            traces,
            (((1,), (1,)), ((), ())),
            preferred_element_type=F32,
        )
        out_ref[j] = chosen[:, :PACKED] + chosen[:, PACKED:]


def one_hot(source, count, base):
    row = lax.broadcasted_iota(jnp.int32, (count, source.shape[1]), 0) + base
    return jnp.where(row == source, 1.0, 0.0).astype(BF16)


def turned(gathered, permutation, turn):
    variants = mm(turn, gathered)
    out = variants[:EXT]
    for p in range(1, 6):
        out = jnp.where(permutation == p, variants[p * EXT : (p + 1) * EXT], out)
    return out


def face_flux(jump, geom_ref, f):
    j = [jump[c * PADDED : (c + 1) * PADDED] for c in range(6)]
    nx, ny, nz, scale = (geom_ref[k, f : f + 1, :] for k in range(4))
    half = 0.5 * scale
    along_h = nx * j[0] + ny * j[1] + nz * j[2]
    along_e = nx * j[3] + ny * j[4] + nz * j[5]
    return [
        (-(ny * j[5] - nz * j[4]) + j[0] - along_h * nx) * half,
        (-(nz * j[3] - nx * j[5]) + j[1] - along_h * ny) * half,
        (-(nx * j[4] - ny * j[3]) + j[2] - along_h * nz) * half,
        (ny * j[2] - nz * j[1] + j[3] - along_e * nx) * half,
        (nz * j[0] - nx * j[2] + j[4] - along_e * ny) * half,
        (nx * j[1] - ny * j[0] + j[5] - along_e * nz) * half,
    ]


def lifted_from(fluxes, lift):
    out = []
    for c in range(6):
        x = jnp.concatenate([fluxes[f][c] for f in range(4)], axis=0)
        out.append(split_product(lift, stacked_values(x)))
    return out


def alive(live_ref, elements):
    return (lax.broadcasted_iota(jnp.int32, (1, elements), 1) < live_ref[0]).astype(F32)


def first_kernel(live_ref, fields_ref, send_ref, pick_ref, out_ref):
    elements = fields_ref.shape[2]
    state = fields_ref[...].reshape(6 * NODES, elements) * alive(live_ref, elements)
    pack(traces_of(state, pick_ref[...]), send_ref[...], out_ref)


def local_kernel(
    masked,
    live_ref,
    state_ref,
    metric_ref,
    geom_ref,
    source_ref,
    permutation_ref,
    derivatives_ref,
    lift_ref,
    pick_ref,
    turn_ref,
    spread_lift_ref,
    spread_node_ref,
    out_ref,
):
    elements = state_ref.shape[2]
    state = state_ref[...].reshape(6 * NODES, elements)
    if masked:
        state = state * alive(live_ref, elements)
    traces = traces_of(state, pick_ref[...])
    fluxes = []
    for f in range(4):
        gathered = mm(traces, one_hot(source_ref[f : f + 1, :], 4 * elements, 0)).astype(BF16)
        exterior = turned(gathered, permutation_ref[f : f + 1, :], turn_ref[...])
        interior = mm(turn_ref[:EXT], traces[:, f * elements : (f + 1) * elements])
        fluxes.append(face_flux(exterior - interior, geom_ref, f))
    lifted = lifted_from(fluxes, stacked_weights(lift_ref[...], spread_lift_ref))
    nabla = stacked_weights(derivatives_ref[...].reshape(3 * NODES, NODES), spread_node_ref)
    rate = lifted
    for c in range(6):
        slopes = split_product(nabla, stacked_values(state[c * NODES : (c + 1) * NODES]))
        s0, s1, s2 = (slopes[m * NODES : (m + 1) * NODES] for m in range(3))

        def gradient(x):
            return (
                metric_ref[x : x + 1] * s0
                + metric_ref[3 + x : 4 + x] * s1
                + metric_ref[6 + x : 7 + x] * s2
            )

        first, second = (c + 1) % 3, (c + 2) % 3
        base = 0 if c >= 3 else 3
        sign = -1.0 if c >= 3 else 1.0
        rate[base + first] = rate[base + first] + sign * gradient(second)
        rate[base + second] = rate[base + second] - sign * gradient(first)
    for c in range(6):
        out_ref[c] = rate[c]


def received_lift(ghost_refs, geom_ref, source_ref, permutation_ref, lift_ref, turn_ref, spread_ref):
    elements = source_ref.shape[1]
    columns = []
    for ref in ghost_refs:
        high, low = halves(jnp.transpose(ref, (1, 0)))
        columns.append(jnp.concatenate([high, low], axis=0))
    table = jnp.concatenate(columns, axis=1)
    fluxes = []
    for f in range(4):
        chosen = one_hot(source_ref[f : f + 1, :], table.shape[1], 4 * elements)
        gathered = mm(table, chosen).astype(BF16)
        exterior = turned(gathered, permutation_ref[f : f + 1, :], turn_ref[...])
        fluxes.append(face_flux(exterior, geom_ref, f))
    return lifted_from(fluxes, stacked_weights(lift_ref[...], spread_ref))


def final_kernel(
    step,
    live_ref,
    state_ref,
    residual_ref,
    partial_ref,
    down_ref,
    swapped_ref,
    up_ref,
    geom_ref,
    source_ref,
    permutation_ref,
    ratio_ref,
    curved_ref,
    lift_ref,
    turn_ref,
    spread_lift_ref,
    pick_ref,
    send_ref,
    *out_refs,
):
    elements = state_ref.shape[2]
    slots = swapped_ref.shape[1] // 3
    ghosts = [
        down_ref[...].reshape(-1, PACKED),
        swapped_ref[:, slots : 2 * slots].reshape(-1, PACKED),
        up_ref[...].reshape(-1, PACKED),
    ]
    lifted = received_lift(
        ghosts, geom_ref, source_ref, permutation_ref, lift_ref, turn_ref, spread_lift_ref
    )
    mask = alive(live_ref, elements)
    scaling = jnp.where(curved_ref[...] == 1, ratio_ref[...], 1.0) * mask
    state_out, residual_out = out_refs[:2]
    advanced = []
    for c in range(6):
        rate = (partial_ref[c] + lifted[c]) * scaling
        state = state_ref[c]
        if step == 0:
            state = state * mask
            residual = TIME_STEP * rate
        else:
            residual = RK_A[step] * residual_ref[c] + TIME_STEP * rate
        state = state + RK_B[step] * residual
        state_out[c] = state
        residual_out[c] = residual
        advanced.append(state)
    if step == 0:
        pack(
            traces_of(jnp.concatenate(advanced, axis=0), pick_ref[...]), send_ref[...], out_refs[2]
        )


VMEM = pl.BlockSpec(memory_space=pltpu.VMEM)
SMEM = pl.BlockSpec(memory_space=pltpu.SMEM)


def call(kernel, count, out_shape, name, flops):
    return pl.pallas_call(
        kernel,
        out_shape=out_shape,
        in_specs=[SMEM] + [VMEM] * count,
        out_specs=jax.tree.map(lambda _: VMEM, out_shape),
        compiler_params=pltpu.CompilerParams(vmem_limit_bytes=48 * 1024 * 1024),
        cost_estimate=pl.CostEstimate(flops=flops, bytes_accessed=4_000_000, transcendentals=0),
        name=name,
    )


def on_device(
    fields,
    metric,
    face_geom,
    jacobian_ratio,
    curved,
    derivatives,
    lift_matrix,
    live_count,
    send_list,
    face_source,
    face_permutation,
):
    elements = fields.shape[2]
    pick, turn, spread_lift, spread_node = (jnp.asarray(a) for a in constant_matrices())
    slots = send_list.shape[3]
    send = send_list.reshape(24, slots)
    curved_row = curved.reshape(1, elements)
    whole = jax.ShapeDtypeStruct((6, NODES, elements), F32)
    outgoing_shape = jax.ShapeDtypeStruct((8, 3 * slots, PACKED), F32)

    outgoing = call(first_kernel, 3, outgoing_shape, "first", 1_000_000_000)(
        live_count, fields, send, pick
    )
    current, residual = fields, fields
    for step in range(2):
        swapped = lax.all_to_all(outgoing, "sub", split_axis=0, concat_axis=0, tiled=True)
        partial = call(
            functools.partial(local_kernel, step == 0), 11, whole, "local", 3_000_000_000
        )(
            live_count,
            current,
            metric,
            face_geom,
            face_source,
            face_permutation,
            derivatives,
            lift_matrix,
            pick,
            turn,
            spread_lift,
            spread_node,
        )
        down = passed_along(swapped[:, :slots], "dom", -1)
        up = passed_along(swapped[:, 2 * slots :], "dom", 1)
        shapes = [whole, whole] + ([outgoing_shape] if step == 0 else [])
        current, residual, *rest = call(
            functools.partial(final_kernel, step), 16, shapes, "final", 3_000_000_000
        )(
            live_count,
            current,
            residual,
            partial,
            down,
            swapped,
            up,
            face_geom,
            face_source,
            face_permutation,
            jacobian_ratio,
            curved_row,
            lift_matrix,
            turn,
            spread_lift,
            pick,
            send,
        )
        if rest:
            outgoing = rest[0]
    return (current, residual)


def solution(mesh):
    return jax.shard_map(
        on_device,
        mesh=mesh,
        in_specs=(
            P(None, None, ("dom", "sub")),
            P(None, ("dom", "sub")),
            P(None, None, ("dom", "sub")),
            P(None, ("dom", "sub")),
            P(("dom", "sub")),
            P(),
            P(),
            P(("dom", "sub")),
            P(("dom", "sub"), None, None, None),
            P(None, ("dom", "sub")),
            P(None, ("dom", "sub")),
        ),
        out_specs=(P(None, None, ("dom", "sub")), P(None, None, ("dom", "sub"))),
        check_vma=False,
    )
```

time: 347 us -> 65.8 us (0.19)
  the two profiles are of different devices: /device:TPU:384 before, /device:TPU:248 now
where the time goes in v1:
time: 65.8 us; the launch traced here: 65.3 us
  blocking collectives  24.5 us (37%)
  Pallas kernels  15.4 us (23%)
  starting transfers between devices  12.7 us (19%)
  waiting for transfers between devices  8.36 us (13%)
  local copies, waits for them, and re-layouts  2.78 us (4%)
  between operations  1.52 us (2%)
    all_to_all x2, blocking collectives, on_device(): lax.all_to_all(outgoing, 'sub', split_axis=0, concat_axis=0, tiled=True)  24.5 us
    ppermute x4, starting transfers between devices, passed_along(): return lax.ppermute(array, axis, pairs)  12.7 us
    ppermute x4, waiting for transfers between devices, passed_along(): return lax.ppermute(array, axis, pairs)  8.36 us
    pallas_call x2, Pallas kernels, on_device(): call(functools.partial(local_kernel, step == 0), 11, whole, 'local', 3000...  7.65 us
    pallas_call x2, Pallas kernels, on_device(): call(functools.partial(final_kernel, step), 16, shapes, 'final', 3000000000)  6.05 us
    unnamed x30, local copies, waits for them, and re-layouts  2.74 us
    pallas_call x1, Pallas kernels, on_device(): call(first_kernel, 3, outgoing_shape, 'first', 1000000000)  1.72 us
  transfers between devices with their start and end apart: 4, of which 2 were waited for; matrix products, arithmetic and copies ran while one was open for 0% of the time, Pallas kernels for 12%

profile of v1, /device:TPU:248, one launch (start us, length us, event | category | flops | bytes accessed | tf_op | source)
XLA Modules:
  0.0 65.3 jit_solution(6142803852742974740)
XLA Ops:
  1.3 0.0 copy-start
  1.3 1.0 %copy-done = f32[6,56,256]{2,1,0:T(8,128)S(1)} copy-done((f32[6,56,256]{2,1,0:T(8,128)S(1)}, f32[6,56,256]{2,1,0:T(8,128)}, u32[]{:S(2)}) %copy-start) | copy-done | bytes 344088
  2.3 0.0 copy-start.6
  2.3 0.7 %copy-done.6 = s32[1,3,8,32]{3,2,1,0:T(8,128)S(1)} copy-done((s32[1,3,8,32]{3,2,1,0:T(8,128)S(1)}, s32[1,3,8,32]{3,2,1,0:T(8,128)}, u32[]{:S(2)}) %copy-start.6) | copy-done | bytes 3096
  3.0 0.0 copy-start.12
  3.0 1.0 %copy-done.12 = bf16[512,336]{1,0:T(8,128)(2,1)S(1)} copy-done((bf16[512,336]{1,0:T(8,128)(2,1)S(1)}, bf16[512,336]{1,0:T(8,128)(2,1)}, u32[]{:S(2)}) %copy-start.12) | copy-done | bytes 344088
  4.0 1.7 %first.1 = f32[8,96,128]{2,1,0:T(8,128)S(1)} custom-call(s32[1]{0:T(128)S(6)} %copy.17.live_ref, f32[6,56,256]{2,1,0:T(8,128)S(1)} %copy-done, s32[24,32]{1,0:T(8,128)S(1)} %bitcast.2, bf16[512,336]{1,0:T(8,128)(2,1)S(1)} %copy-done.12), custom_call_target="tpu_custom_call" | custom-call | flops 1000000000 | bytes 4000000 | tf_op jit(solution)/shard_map/first/pallas_call | solution.py:338
  5.7 0.0 copy-start.11
  5.7 13.2 %all_to_all.10.swapped_ref = f32[8,96,128]{2,1,0:T(8,128)S(1)} all-to-all(f32[8,96,128]{2,1,0:T(8,128)S(1)} %first.1), channel_id=1, replica_groups=mesh['dom'=64,'sub'=8] {'sub'}, dimensions={0} | all-to-all | bytes 786432 | tf_op jit(solution)/shard_map/all_to_all | solution.py:343
  18.9 0.0 copy-start.1
  18.9 0.0 copy-start.3
  18.9 0.0 copy-start.4
  18.9 0.0 copy-start.5
  18.9 0.0 copy-start.8
  18.9 0.0 copy-start.9
  18.9 0.0 copy-start.13
  18.9 0.0 copy-start.14
  19.0 4.8 %collective-permute-start.1 = (f32[8,32,128]{2,1,0:T(8,128)S(1)}, f32[8,32,128]{2,1,0:T(8,128)S(1)}, u32[]{:S(2)}, u32[]{:S(2)}) collective-permute-start(f32[8,32,128]{2,1,0:T(8,128)S(1)} %get-tuple-element.10), channel_id=1, source_target_pairs={{0,8},{8,16},{16,24},{24,32},{32,40},{40,48},{48,56},{56,64},{64,7... | collective-permute-start | bytes 393224 | tf_op jit(solution)/shard_map/ppermute | solution.py:29
  23.8 0.0 copy-start.2
  23.8 0.0 copy-start.7
  23.8 2.1 %collective-permute-start = (f32[8,32,128]{2,1,0:T(8,128)S(1)}, f32[8,32,128]{2,1,0:T(8,128)S(1)}, u32[]{:S(2)}, u32[]{:S(2)}) collective-permute-start(f32[8,32,128]{2,1,0:T(8,128)S(1)} %get-tuple-element.11), channel_id=1, source_target_pairs={{8,0},{16,8},{24,16},{32,24},{40,32},{48,40},{56,48},{64,56},{72,6... | collective-permute-start | bytes 393224 | tf_op jit(solution)/shard_map/ppermute | solution.py:29
  25.9 0.0 copy-done.11
  25.9 0.0 copy-done.1
  25.9 0.0 copy-done.3
  25.9 0.0 copy-done.4
  25.9 0.0 copy-done.5
  25.9 0.0 copy-done.8
  25.9 0.0 copy-done.9
  26.0 0.0 copy-done.13
  26.0 0.0 copy-done.14
  26.0 3.8 %local.2.partial_ref = f32[6,56,256]{2,1,0:T(8,128)S(1)} custom-call(s32[1]{0:T(128)S(6)} %copy.17.live_ref, f32[6,56,256]{2,1,0:T(8,128)S(1)} %copy-done, f32[9,256]{1,0:T(8,128)S(1)} %copy-done.4, f32[4,4,256]{2,1,0:T(4,128)S(1)} %copy-done.5, s32[4,256]{1,0:T(4,128)S(1)} %copy-done.8, s32[4,256]{1,0:T(4,128)S(1)} %copy-done.9, ...), custom_call_target="tpu_custom_call" | custom-call | flops 3000000000 | bytes 4000000 | tf_op jit(solution)/shard_map/local/pallas_call | solution.py:344
  29.8 0.0 copy-start.10
  29.8 0.0 collective-permute-done.1.up_ref
  29.8 4.3 %collective-permute-done.down_ref = f32[8,32,128]{2,1,0:T(8,128)S(1)} collective-permute-done((f32[8,32,128]{2,1,0:T(8,128)S(1)}, f32[8,32,128]{2,1,0:T(8,128)S(1)}, u32[]{:S(2)}, u32[]{:S(2)}) %collective-permute-start) | collective-permute-done | bytes 131104 | tf_op jit(solution)/shard_map/ppermute | solution.py:29
  34.1 0.0 copy-done.2
  34.1 0.0 copy-done.7
  34.1 0.0 copy-done.10
  34.1 3.4 %final.2 = (f32[6,56,256]{2,1,0:T(8,128)S(1)}, f32[6,56,256]{2,1,0:T(8,128)S(1)}, f32[8,96,128]{2,1,0:T(8,128)S(1)}) custom-call(s32[1]{0:T(128)S(6)} %copy.17.live_ref, f32[6,56,256]{2,1,0:T(8,128)S(1)} %copy-done, f32[6,56,256]{2,1,0:T(8,128)S(1)} %copy-done, f32[6,56,256]{2,1,0:T(8,128)S(1)} %local.2.partial_ref, ...), custom_call_target="tpu_custom_call" | custom-call | flops 3000000000 | bytes 4000000 | tf_op jit(solution)/shard_map/final/pallas_call | solution.py:363
  37.6 11.3 %all_to_all.11.swapped_ref = f32[8,96,128]{2,1,0:T(8,128)S(1)} all-to-all(f32[8,96,128]{2,1,0:T(8,128)S(1)} %get-tuple-element.7), channel_id=1, replica_groups=mesh['dom'=64,'sub'=8] {'sub'}, dimensions={0} | all-to-all | bytes 786432 | tf_op jit(solution)/shard_map/all_to_all | solution.py:343
  49.0 3.6 %collective-permute-start.3 = (f32[8,32,128]{2,1,0:T(8,128)S(1)}, f32[8,32,128]{2,1,0:T(8,128)S(1)}, u32[]{:S(2)}, u32[]{:S(2)}) collective-permute-start(f32[8,32,128]{2,1,0:T(8,128)S(1)} %get-tuple-element.8), channel_id=1, source_target_pairs={{0,8},{8,16},{16,24},{24,32},{32,40},{40,48},{48,56},{56,64},{64,7... | collective-permute-start | bytes 393224 | tf_op jit(solution)/shard_map/ppermute | solution.py:29
  52.5 2.3 %collective-permute-start.2 = (f32[8,32,128]{2,1,0:T(8,128)S(1)}, f32[8,32,128]{2,1,0:T(8,128)S(1)}, u32[]{:S(2)}, u32[]{:S(2)}) collective-permute-start(f32[8,32,128]{2,1,0:T(8,128)S(1)} %get-tuple-element.9), channel_id=1, source_target_pairs={{8,0},{16,8},{24,16},{32,24},{40,32},{48,40},{56,48},{64,56},{72,6... | collective-permute-start | bytes 393224 | tf_op jit(solution)/shard_map/ppermute | solution.py:29
  54.8 3.8 %local.3.partial_ref = f32[6,56,256]{2,1,0:T(8,128)S(1)} custom-call(s32[1]{0:T(128)S(6)} %copy.17.live_ref, f32[6,56,256]{2,1,0:T(8,128)S(1)} %get-tuple-element.5.state_ref, f32[9,256]{1,0:T(8,128)S(1)} %copy-done.4, f32[4,4,256]{2,1,0:T(4,128)S(1)} %copy-done.5, s32[4,256]{1,0:T(4,128)S(1)} %copy-done.8, s32[4,256]{1,0:T(4,128)S(1)} %copy-done.9, ...), custom_call_target="tpu_custom_call" | custom-call | flops 3000000000 | bytes 4000000 | tf_op jit(solution)/shard_map/local/pallas_call | solution.py:344
  58.6 0.0 collective-permute-done.3.up_ref
  58.6 4.0 %collective-permute-done.2.down_ref = f32[8,32,128]{2,1,0:T(8,128)S(1)} collective-permute-done((f32[8,32,128]{2,1,0:T(8,128)S(1)}, f32[8,32,128]{2,1,0:T(8,128)S(1)}, u32[]{:S(2)}, u32[]{:S(2)}) %collective-permute-start.2) | collective-permute-done | bytes 131104 | tf_op jit(solution)/shard_map/ppermute | solution.py:29
  62.7 2.6 %final.3 = (f32[6,56,256]{2,1,0:T(8,128)}, f32[6,56,256]{2,1,0:T(8,128)}) custom-call(s32[1]{0:T(128)S(6)} %copy.17.live_ref, f32[6,56,256]{2,1,0:T(8,128)S(1)} %get-tuple-element.5.state_ref, f32[6,56,256]{2,1,0:T(8,128)S(1)} %get-tuple-element.6.residual_ref, f32[6,56,256]{2,1,0:T(8,128)S(1)} %local.3.partial_ref, ...), custom_call_target="tpu_custom_call" | custom-call | flops 3000000000 | bytes 4000000 | tf_op jit(solution)/shard_map/final/pallas_call | solution.py:363
  (2 shorter events, 0.0 us)
Async XLA Ops:
  1.3 1.0 %copy-start = (f32[6,56,256]{2,1,0:T(8,128)S(1)}, f32[6,56,256]{2,1,0:T(8,128)}, u32[]{:S(2)}) copy-start(f32[6,56,256]{2,1,0:T(8,128)} %residual_ref.1) | copy-start | bytes 1032196
  2.3 0.7 %copy-start.6 = (s32[1,3,8,32]{3,2,1,0:T(8,128)S(1)}, s32[1,3,8,32]{3,2,1,0:T(8,128)}, u32[]{:S(2)}) copy-start(s32[1,3,8,32]{3,2,1,0:T(8,128)} %param.23) | copy-start | bytes 9220
  3.0 1.0 %copy-start.12 = (bf16[512,336]{1,0:T(8,128)(2,1)S(1)}, bf16[512,336]{1,0:T(8,128)(2,1)}, u32[]{:S(2)}) copy-start(bf16[512,336]{1,0:T(8,128)(2,1)} %constant.8.clone.pick_ref) | copy-start | bytes 1032196
  5.7 20.2 %copy-start.11 = (bf16[864,256]{1,0:T(8,128)(2,1)S(1)}, bf16[864,256]{1,0:T(8,128)(2,1)}, u32[]{:S(2)}) copy-start(bf16[864,256]{1,0:T(8,128)(2,1)} %constant.9.clone.turn_ref) | copy-start | bytes 1327108
  18.9 7.0 %copy-start.1 = (f32[3,56,56]{2,1,0:T(8,128)S(1)}, f32[3,56,56]{2,1,0:T(8,128)}, u32[]{:S(2)}) copy-start(f32[3,56,56]{2,1,0:T(8,128)} %derivatives_ref.3) | copy-start | bytes 112900
  18.9 7.0 %copy-start.3 = (f32[56,84]{1,0:T(8,128)S(1)}, f32[56,84]{1,0:T(8,128)}, u32[]{:S(2)}) copy-start(f32[56,84]{1,0:T(8,128)} %lift_ref.7) | copy-start | bytes 56452
  18.9 7.0 %copy-start.4 = (f32[9,256]{1,0:T(8,128)S(1)}, f32[9,256]{1,0:T(8,128)}, u32[]{:S(2)}) copy-start(f32[9,256]{1,0:T(8,128)} %metric_ref.3) | copy-start | bytes 27652
  18.9 7.0 %copy-start.5 = (f32[4,4,256]{2,1,0:T(4,128)S(1)}, f32[4,4,256]{2,1,0:T(4,128)}, u32[]{:S(2)}) copy-start(f32[4,4,256]{2,1,0:T(4,128)} %geom_ref.7) | copy-start | bytes 49156
  18.9 7.1 %copy-start.8 = (s32[4,256]{1,0:T(4,128)S(1)}, s32[4,256]{1,0:T(4,128)}, u32[]{:S(2)}) copy-start(s32[4,256]{1,0:T(4,128)} %source_ref.7) | copy-start | bytes 12292
  18.9 7.0 %copy-start.9 = (s32[4,256]{1,0:T(4,128)S(1)}, s32[4,256]{1,0:T(4,128)}, u32[]{:S(2)}) copy-start(s32[4,256]{1,0:T(4,128)} %permutation_ref.7) | copy-start | bytes 12292
  18.9 7.0 %copy-start.13 = (bf16[2,84,192]{2,1,0:T(8,128)(2,1)S(1)}, bf16[2,84,192]{2,1,0:T(8,128)(2,1)}, u32[]{:S(2)}) copy-start(bf16[2,84,192]{2,1,0:T(8,128)(2,1)} %constant.10.clone.spread_lift_ref) | copy-start | bytes 193540
  18.9 7.0 %copy-start.14 = (bf16[2,56,112]{2,1,0:T(8,128)(2,1)S(1)}, bf16[2,56,112]{2,1,0:T(8,128)(2,1)}, u32[]{:S(2)}) copy-start(bf16[2,56,112]{2,1,0:T(8,128)(2,1)} %constant.11.clone.spread_node_ref) | copy-start | bytes 75268
  19.0 10.9 %collective-permute-start.1 = (f32[8,32,128]{2,1,0:T(8,128)S(1)}, f32[8,32,128]{2,1,0:T(8,128)S(1)}, u32[]{:S(2)}, u32[]{:S(2)}) collective-permute-start(f32[8,32,128]{2,1,0:T(8,128)S(1)} %get-tuple-element.10), channel_id=1, source_target_pairs={{0,8},{8,16},{16,24},{24,32},{32,40},{40,48},{48,56},{56,64},{64,7... | collective-permute-start | bytes 393224 | tf_op jit(solution)/shard_map/ppermute | solution.py:29
  23.8 10.3 %copy-start.2 = (f32[56,256]{1,0:T(8,128)S(1)}, f32[56,256]{1,0:T(8,128)}, u32[]{:S(2)}) copy-start(f32[56,256]{1,0:T(8,128)} %ratio_ref.3) | copy-start | bytes 172036
  23.8 10.3 %copy-start.7 = (s32[1,3,8,32]{3,2,1,0:T(8,128)S(1)}, s32[1,3,8,32]{3,2,1,0:T(8,128)}, u32[]{:S(2)}) copy-start(s32[1,3,8,32]{3,2,1,0:T(8,128)} %param.23) | copy-start | bytes 9220
  23.8 10.3 %collective-permute-start = (f32[8,32,128]{2,1,0:T(8,128)S(1)}, f32[8,32,128]{2,1,0:T(8,128)S(1)}, u32[]{:S(2)}, u32[]{:S(2)}) collective-permute-start(f32[8,32,128]{2,1,0:T(8,128)S(1)} %get-tuple-element.11), channel_id=1, source_target_pairs={{8,0},{16,8},{24,16},{32,24},{40,32},{48,40},{56,48},{64,56},{72,6... | collective-permute-start | bytes 393224 | tf_op jit(solution)/shard_map/ppermute | solution.py:29
  29.8 4.3 %copy-start.10 = (s32[256]{0:T(256)S(1)}, s32[256]{0:T(256)}, u32[]{:S(2)}) copy-start(s32[256]{0:T(256)} %param.19) | copy-start | bytes 3076
  49.0 9.7 %collective-permute-start.3 = (f32[8,32,128]{2,1,0:T(8,128)S(1)}, f32[8,32,128]{2,1,0:T(8,128)S(1)}, u32[]{:S(2)}, u32[]{:S(2)}) collective-permute-start(f32[8,32,128]{2,1,0:T(8,128)S(1)} %get-tuple-element.8), channel_id=1, source_target_pairs={{0,8},{8,16},{16,24},{24,32},{32,40},{40,48},{48,56},{56,64},{64,7... | collective-permute-start | bytes 393224 | tf_op jit(solution)/shard_map/ppermute | solution.py:29
  52.5 10.2 %collective-permute-start.2 = (f32[8,32,128]{2,1,0:T(8,128)S(1)}, f32[8,32,128]{2,1,0:T(8,128)S(1)}, u32[]{:S(2)}, u32[]{:S(2)}) collective-permute-start(f32[8,32,128]{2,1,0:T(8,128)S(1)} %get-tuple-element.9), channel_id=1, source_target_pairs={{8,0},{16,8},{24,16},{32,24},{40,32},{48,40},{56,48},{64,56},{72,6... | collective-permute-start | bytes 393224 | tf_op jit(solution)/shard_map/ppermute | solution.py:29

commit v2 on v1

v2 whole, which is shorter than its diff:
```python
import functools

import jax
import jax.numpy as jnp
import ml_dtypes
import numpy as np
from jax import lax
from jax.experimental import pallas as pl
from jax.experimental.pallas import tpu as pltpu
from jax.sharding import PartitionSpec as P

RK_A = (0.0, -567301805773.0 / 1357537059087.0)
RK_B = (1432997174477.0 / 9575080441755.0, 5161836677717.0 / 13612068292357.0)
TIME_STEP = 0.5
SYMMETRIES = ((0, 1, 2), (1, 2, 0), (2, 0, 1), (0, 2, 1), (2, 1, 0), (1, 0, 2))

NODES = 56
TRACE = 21
PADDED = 24
PACKED = 128
EXT = 6 * PADDED
HALF = 3 * PADDED
F32 = jnp.float32
BF16 = jnp.bfloat16


def swapped_pairs(array, axis, first):
    count = lax.axis_size(axis)
    pairs = []
    for low in range(first, count - 1, 2):
        pairs += [(low, low + 1), (low + 1, low)]
    return lax.ppermute(array, axis, pairs)


def node_tables():
    volume_nodes = [(i, j, k) for i in range(6) for j in range(6 - i) for k in range(6 - i - j)]
    volume_index = {v: n for n, v in enumerate(volume_nodes)}
    triangle = [(a, b) for a in range(6) for b in range(6 - a)]
    triangle_index = {t: n for n, t in enumerate(triangle)}
    face_nodes = np.array(
        [
            [volume_index[a, b, 0] for a, b in triangle],
            [volume_index[a, 0, b] for a, b in triangle],
            [volume_index[a, b, 5 - a - b] for a, b in triangle],
            [volume_index[0, a, b] for a, b in triangle],
        ],
        np.int32,
    )
    permuted = np.array(
        [
            [triangle_index[(a, b, 5 - a - b)[q[0]], (a, b, 5 - a - b)[q[1]]] for a, b in triangle]
            for q in SYMMETRIES
        ],
        np.int32,
    )
    return (face_nodes, permuted)


def constant_matrices():
    face_nodes, permuted = node_tables()
    pick = np.zeros((4 * PACKED, 6 * NODES), np.float32)
    pad = np.zeros((EXT, 2 * PACKED), np.float32)
    turn = np.zeros((6 * HALF, 2 * HALF), np.float32)
    for m in range(TRACE):
        for c in range(6):
            for f in range(4):
                pick[f * PACKED + c * TRACE + m, c * NODES + face_nodes[f, m]] = 1
            for part in range(2):
                pad[c * PADDED + m, part * PACKED + c * TRACE + m] = 1
        for c in range(3):
            for p in range(6):
                for part in range(2):
                    turn[p * HALF + c * PADDED + m, part * HALF + c * PADDED + permuted[p, m]] = 1
    spread_lift = np.zeros((2, 4 * TRACE, 8 * PADDED), np.float32)
    for f in range(4):
        for m in range(TRACE):
            spread_lift[0, f * TRACE + m, f * PADDED + m] = 1
            spread_lift[0, f * TRACE + m, (4 + f) * PADDED + m] = 1
            spread_lift[1, f * TRACE + m, f * PADDED + m] = 1
    spread_node = np.zeros((2, NODES, 2 * NODES), np.float32)
    spread_node[0, :, :NODES] = spread_node[0, :, NODES:] = np.eye(NODES)
    spread_node[1, :, :NODES] = np.eye(NODES)
    return [a.astype(ml_dtypes.bfloat16) for a in (pick, pad, turn, spread_lift, spread_node)]


def mm(a, b):
    return jnp.dot(a, b, preferred_element_type=F32)


def halves(x):
    high = x.astype(BF16)
    return high, (x - high.astype(F32)).astype(BF16)


def stacked_weights(weights, spread):
    high, low = halves(weights)
    return jnp.concatenate([mm(high, spread[0]), mm(low, spread[1])], axis=0).astype(BF16)


def stacked_values(x):
    high = x.astype(BF16).astype(F32)
    return jnp.concatenate([high, x - high], axis=0).astype(BF16)


def split_product(weights, values):
    both = mm(weights, values)
    rows = both.shape[0] // 2
    return both[:rows] + both[rows:]


def traces_of(state, pick):
    high, low = halves(state)
    parts = []
    for part in (high, low):
        all_faces = mm(pick, part).astype(BF16)
        parts.append(
            jnp.concatenate([all_faces[f * PACKED : (f + 1) * PACKED] for f in range(4)], axis=1)
        )
    return jnp.concatenate(parts, axis=0)


def even_group():
    return lax.rem(lax.axis_index("dom"), 2) == 0


def outgoing_choice(send, faces):
    even = even_group()
    low, own, high = send[:8], send[8:16], send[16:]
    ordered = [jnp.where(even, high, low), own, jnp.where(even, low, high)]
    columns = jnp.transpose(jnp.concatenate(ordered, axis=0), (1, 0))
    lane = lax.broadcasted_iota(jnp.int32, (send.shape[1], faces), 1)
    rows = []
    for j in range(8):
        for block in range(3):
            r = block * 8 + j
            rows.append(jnp.where(lane == columns[:, r : r + 1], 1.0, 0.0).astype(BF16))
    return jnp.concatenate(rows, axis=0)


def pack(choice, traces, out_ref):
    chosen = lax.dot_general(
        choice, traces, (((1,), (1,)), ((), ())), preferred_element_type=F32
    )
    out_ref[...] = (chosen[:, :PACKED] + chosen[:, PACKED:]).reshape(out_ref.shape)


def one_hot(source, count, base):
    row = lax.broadcasted_iota(jnp.int32, (count, source.shape[1]), 0) + base
    return jnp.where(row == source, 1.0, 0.0).astype(BF16)


def row_of_faces(ref, lead=()):
    return jnp.concatenate([ref[lead + (slice(f, f + 1),)] for f in range(4)], axis=1)


def flux_h(traces, n, half):
    j = [traces[c * PADDED : (c + 1) * PADDED] for c in range(6)]
    along = n[0] * j[0] + n[1] * j[1] + n[2] * j[2]
    parts = [
        (-(n[1] * j[5] - n[2] * j[4]) + j[0] - along * n[0]) * half,
        (-(n[2] * j[3] - n[0] * j[5]) + j[1] - along * n[1]) * half,
        (-(n[0] * j[4] - n[1] * j[3]) + j[2] - along * n[2]) * half,
    ]
    return jnp.concatenate(parts, axis=0)


def turned(flux, permutation, turn):
    variants = mm(turn, stacked_values(flux))
    out = variants[:HALF]
    for p in range(1, 6):
        out = jnp.where(permutation == p, variants[p * HALF : (p + 1) * HALF], out)
    return out


def lifted_from(flux, n, lift):
    h = [flux[c * PADDED : (c + 1) * PADDED] for c in range(3)]
    e = [n[(c + 1) % 3] * h[(c + 2) % 3] - n[(c + 2) % 3] * h[(c + 1) % 3] for c in range(3)]
    elements = flux.shape[1] // 4
    out = []
    for x in h + e:
        x = jnp.concatenate([x[:, f * elements : (f + 1) * elements] for f in range(4)], axis=0)
        out.append(split_product(lift, stacked_values(x)))
    return out


def normals(geom_ref):
    n = [row_of_faces(geom_ref, (k,)) for k in range(4)]
    return n[:3], 0.5 * n[3]


def alive(live_ref, elements):
    return (lax.broadcasted_iota(jnp.int32, (1, elements), 1) < live_ref[0]).astype(F32)


def first_kernel(
    live_ref,
    fields_hbm,
    send_hbm,
    pick_hbm,
    out_ref,
    choice_ref,
    state_ref,
    traces_ref,
    fields_ref,
    send_ref,
    pick_ref,
    sems,
):
    elements = fields_ref.shape[2]
    send_copy = pltpu.make_async_copy(send_hbm, send_ref, sems.at[0])
    fields_copy = pltpu.make_async_copy(fields_hbm, fields_ref, sems.at[1])
    pick_copy = pltpu.make_async_copy(pick_hbm, pick_ref, sems.at[2])
    send_copy.start()
    fields_copy.start()
    pick_copy.start()
    send_copy.wait()
    choice_ref[...] = outgoing_choice(send_ref[...], 4 * elements)
    fields_copy.wait()
    state = fields_ref[...].reshape(6 * NODES, elements) * alive(live_ref, elements)
    state_ref[...] = state.reshape(state_ref.shape)
    pick_copy.wait()
    traces = traces_of(state, pick_ref[...])
    traces_ref[...] = traces
    pack(choice_ref[...], traces, out_ref)


def local_kernel(
    step,
    live_ref,
    state_ref,
    traces_ref,
    metric_ref,
    geom_ref,
    source_ref,
    permutation_ref,
    derivatives_ref,
    lift_ref,
    pad_ref,
    turn_ref,
    spread_lift_ref,
    spread_node_ref,
    ratio_ref,
    curved_ref,
    out_ref,
    *prepared,
):
    elements = state_ref.shape[2]
    n, half = normals(geom_ref)
    source, permutation = row_of_faces(source_ref), row_of_faces(permutation_ref)
    lift = stacked_weights(lift_ref[...], spread_lift_ref)
    traces = traces_ref[...]
    gathered = []
    for f in range(4):
        chosen = one_hot(source_ref[f : f + 1], 4 * elements, 0)
        gathered.append(mm(traces, chosen).astype(BF16))
    gathered = jnp.concatenate(gathered, axis=1)
    flux = turned(flux_h(mm(pad_ref[...], gathered), n, half), permutation, turn_ref[...])
    flux = flux - flux_h(mm(pad_ref[...], traces), n, half)
    rate = lifted_from(flux, n, lift)
    nabla = stacked_weights(derivatives_ref[...].reshape(3 * NODES, NODES), spread_node_ref)
    for c in range(6):
        slopes = split_product(nabla, stacked_values(state_ref[c]))
        s0, s1, s2 = (slopes[m * NODES : (m + 1) * NODES] for m in range(3))

        def gradient(x):
            return (
                metric_ref[x : x + 1] * s0
                + metric_ref[3 + x : 4 + x] * s1
                + metric_ref[6 + x : 7 + x] * s2
            )

        first, second = (c + 1) % 3, (c + 2) % 3
        base = 0 if c >= 3 else 3
        sign = -1.0 if c >= 3 else 1.0
        rate[base + first] = rate[base + first] + sign * gradient(second)
        rate[base + second] = rate[base + second] - sign * gradient(first)
    for c in range(6):
        out_ref[c] = rate[c]
    if step == 0:
        choice_ref, lift_out_ref, scaling_ref = prepared
        lift_out_ref[...] = lift
        ratio = jnp.where(curved_ref[...] == 1, ratio_ref[...], 1.0)
        scaling_ref[...] = ratio * alive(live_ref, elements)
        even = even_group()
        block = choice_ref.shape[0] // 2
        start = 4 * elements
        near, far = start, start + 2 * block
        first_base = jnp.where(even, near, far)
        other_base = jnp.where(even, far, near)
        choice_ref[:block] = one_hot(source, block, first_base)
        choice_ref[block:] = one_hot(source, block, other_base)


def received_flux(tables, choice, geom_ref, permutation_ref, pad_ref, turn_ref):
    columns = []
    for table in tables:
        high, low = halves(jnp.transpose(table, (1, 0)))
        columns.append(jnp.concatenate([high, low], axis=0))
    n, half = normals(geom_ref)
    gathered = mm(jnp.concatenate(columns, axis=1), choice).astype(BF16)
    flux = flux_h(mm(pad_ref[...], gathered), n, half)
    return turned(flux, row_of_faces(permutation_ref), turn_ref[...]), n


def own_kernel(
    live_ref,
    partial_ref,
    swapped_ref,
    geom_ref,
    source_ref,
    permutation_ref,
    lift_ref,
    pad_ref,
    turn_ref,
    out_ref,
):
    slots = swapped_ref.shape[1] // 3
    table = swapped_ref[:, slots : 2 * slots].reshape(-1, PACKED)
    count = table.shape[0]
    base = 4 * source_ref.shape[1] + count
    choice = one_hot(row_of_faces(source_ref), count, base)
    flux, n = received_flux([table], choice, geom_ref, permutation_ref, pad_ref, turn_ref)
    lifted = lifted_from(flux, n, lift_ref[...])
    for c in range(6):
        out_ref[c] = partial_ref[c] + lifted[c]


def final_kernel(
    step,
    live_ref,
    state_ref,
    residual_ref,
    partial_ref,
    first_ref,
    other_ref,
    choice_ref,
    geom_ref,
    permutation_ref,
    scaling_ref,
    lift_ref,
    pad_ref,
    turn_ref,
    pick_ref,
    outgoing_choice_ref,
    *out_refs,
):
    tables = [r[...].reshape(-1, PACKED) for r in (first_ref, other_ref)]
    flux, n = received_flux(
        tables, choice_ref[...], geom_ref, permutation_ref, pad_ref, turn_ref
    )
    lifted = lifted_from(flux, n, lift_ref[...])
    scaling = scaling_ref[...]
    state_out, residual_out = out_refs[:2]
    advanced = []
    for c in range(6):
        residual = TIME_STEP * ((partial_ref[c] + lifted[c]) * scaling)
        if step > 0:
            residual = RK_A[step] * residual_ref[c] + residual
        state = state_ref[c] + RK_B[step] * residual
        state_out[c] = state
        residual_out[c] = residual
        advanced.append(state)
    if step == 0:
        traces = traces_of(jnp.concatenate(advanced, axis=0), pick_ref[...])
        out_refs[3][...] = traces
        pack(outgoing_choice_ref[...], traces, out_refs[2])


VMEM = pl.BlockSpec(memory_space=pltpu.VMEM)
SMEM = pl.BlockSpec(memory_space=pltpu.SMEM)
HBM = pl.BlockSpec(memory_space=pltpu.HBM)


def call(kernel, space, count, out_shape, name, flops, scratch=()):
    return pl.pallas_call(
        kernel,
        out_shape=out_shape,
        in_specs=[SMEM] + [space] * count,
        out_specs=jax.tree.map(lambda _: VMEM, out_shape),
        scratch_shapes=scratch,
        compiler_params=pltpu.CompilerParams(vmem_limit_bytes=40 * 1024 * 1024),
        cost_estimate=pl.CostEstimate(flops=flops, bytes_accessed=4_000_000, transcendentals=0),
        name=name,
    )


def on_device(
    fields,
    metric,
    face_geom,
    jacobian_ratio,
    curved,
    derivatives,
    lift_matrix,
    live_count,
    send_list,
    face_source,
    face_permutation,
):
    elements = fields.shape[2]
    pick, pad, turn, spread_lift, spread_node = (jnp.asarray(a) for a in constant_matrices())
    slots = send_list.shape[3]
    send = send_list.reshape(24, slots)
    curved_row = curved.reshape(1, elements)
    shape = jax.ShapeDtypeStruct
    whole = shape((6, NODES, elements), F32)
    outgoing_shape = shape((8, 3 * slots, PACKED), F32)
    traces_shape = shape((2 * PACKED, 4 * elements), BF16)

    outgoing, outgoing_rows, current, traces = call(
        first_kernel,
        HBM,
        3,
        [outgoing_shape, shape((24 * slots, 4 * elements), BF16), whole, traces_shape],
        "first",
        1_000_000_000,
        scratch=[
            pltpu.VMEM(fields.shape, F32),
            pltpu.VMEM(send.shape, jnp.int32),
            pltpu.VMEM(pick.shape, BF16),
            pltpu.SemaphoreType.DMA((3,)),
        ],
    )(live_count, fields, send, pick)
    residual = current
    for step in range(2):
        swapped = lax.all_to_all(outgoing, "sub", split_axis=0, concat_axis=0, tiled=True)
        shapes = [whole]
        if step == 0:
            shapes += [
                shape((16 * slots, 4 * elements), BF16),
                shape((2 * NODES, 8 * PADDED), BF16),
                shape((NODES, elements), F32),
            ]
        partial, *prepared = call(
            functools.partial(local_kernel, step), VMEM, 14, shapes, "local", 4_000_000_000
        )(
            live_count,
            current,
            traces,
            metric,
            face_geom,
            face_source,
            face_permutation,
            derivatives,
            lift_matrix,
            pad,
            turn,
            spread_lift,
            spread_node,
            jacobian_ratio,
            curved_row,
        )
        if step == 0:
            choice, lift, scaling = prepared
        swapped, partial = lax.optimization_barrier((swapped, partial))
        first = swapped_pairs(swapped[:, :slots], "dom", 0)
        other = swapped_pairs(swapped[:, 2 * slots :], "dom", 1)
        partial = call(own_kernel, VMEM, 8, whole, "own", 1_500_000_000)(
            live_count,
            partial,
            swapped,
            face_geom,
            face_source,
            face_permutation,
            lift,
            pad,
            turn,
        )
        shapes = [whole, whole] + ([outgoing_shape, traces_shape] if step == 0 else [])
        current, residual, *rest = call(
            functools.partial(final_kernel, step), VMEM, 14, shapes, "final", 3_000_000_000
        )(
            live_count,
            current,
            residual,
            partial,
            first,
            other,
            choice,
            face_geom,
            face_permutation,
            scaling,
            lift,
            pad,
            turn,
            pick,
            outgoing_rows,
        )
        if rest:
            outgoing, traces = rest
    return (current, residual)


def solution(mesh):
    return jax.shard_map(
        on_device,
        mesh=mesh,
        in_specs=(
            P(None, None, ("dom", "sub")),
            P(None, ("dom", "sub")),
            P(None, None, ("dom", "sub")),
            P(None, ("dom", "sub")),
            P(("dom", "sub")),
            P(),
            P(),
            P(("dom", "sub")),
            P(("dom", "sub"), None, None, None),
            P(None, ("dom", "sub")),
            P(None, ("dom", "sub")),
        ),
        out_specs=(P(None, None, ("dom", "sub")), P(None, None, ("dom", "sub"))),
        check_vma=False,
    )
```

time: 65.8 us -> 64.1 us (0.974)
  the two profiles are of different devices: /device:TPU:248 before, /device:TPU:384 now
where the time goes in v2:
time: 64.1 us; the launch traced here: 63.4 us
  starting transfers between devices  21.7 us (34%)
  Pallas kernels  14.1 us (22%)
  waiting for transfers between devices  14.1 us (22%)
  local copies, waits for them, and re-layouts  11.8 us (18%)
  between operations  1.65 us (3%)
    ppermute x4, starting transfers between devices, swapped_pairs(): return lax.ppermute(array, axis, pairs)  13.9 us
    unnamed x70, local copies, waits for them, and re-layouts  11.8 us
    all_to_all x2, waiting for transfers between devices, on_device(): lax.all_to_all(outgoing, 'sub', split_axis=0, concat_axis=0, tiled=True)  8.29 us
    all_to_all x2, starting transfers between devices, on_device(): lax.all_to_all(outgoing, 'sub', split_axis=0, concat_axis=0, tiled=True)  7.76 us
    ppermute x4, waiting for transfers between devices, swapped_pairs(): return lax.ppermute(array, axis, pairs)  5.79 us
    pallas_call x2, Pallas kernels, on_device(): call(functools.partial(final_kernel, step), VMEM, 14, shapes, 'final', 30...  5 us
    pallas_call x2, Pallas kernels, on_device(): call(functools.partial(local_kernel, step), VMEM, 14, shapes, 'local', 40...  4.38 us
    pallas_call x1, Pallas kernels, on_device(): call(first_kernel, HBM, 3, [outgoing_shape, shape((24 * slots, 4 * elemen...  2.51 us
  transfers between devices with their start and end apart: 6, of which 5 were waited for; matrix products, arithmetic and copies ran while one was open for 0% of the time, Pallas kernels for 10%

profile of v2, /device:TPU:384, one launch (start us, length us, event | category | flops | bytes accessed | tf_op | source)
XLA Modules:
  0.0 63.4 jit_solution(7971021949281371147)
XLA Ops:
  1.3 1.0 %copy-done = f32[6,56,256]{2,1,0:T(8,128)S(1)} copy-done((f32[6,56,256]{2,1,0:T(8,128)S(1)}, f32[6,56,256]{2,1,0:T(8,128)}, u32[]{:S(2)}) %copy-start) | copy-done | bytes 344088
  2.3 0.7 %copy-done.6 = s32[1,3,8,32]{3,2,1,0:T(8,128)S(1)} copy-done((s32[1,3,8,32]{3,2,1,0:T(8,128)S(1)}, s32[1,3,8,32]{3,2,1,0:T(8,128)}, u32[]{:S(2)}) %copy-start.6) | copy-done | bytes 3096
  3.0 1.0 %copy-done.10 = bf16[512,336]{1,0:T(8,128)(2,1)S(1)} copy-done((bf16[512,336]{1,0:T(8,128)(2,1)S(1)}, bf16[512,336]{1,0:T(8,128)(2,1)}, u32[]{:S(2)}) %copy-start.10) | copy-done | bytes 344088
  4.0 0.0 copy-start.12
  4.0 0.0 copy-start.13
  4.0 0.0 copy-start.14
  4.1 0.0 copy-start.15
  4.1 2.5 %first.1 = (f32[8,96,128]{2,1,0:T(8,128)}, bf16[768,1024]{1,0:T(8,128)(2,1)S(1)}, f32[6,56,256]{2,1,0:T(8,128)S(1)}, bf16[256,1024]{1,0:T(8,128)(2,1)S(1)}) custom-call(s32[1]{0:T(128)S(6)} %copy.18.live_ref, f32[6,56,256]{2,1,0:T(8,128)S(1)} %copy-done, s32[24,32]{1,0:T(8,128)S(1)} %bitcast.2, bf16[512,336]{1,0:T(8,128)(2,1)S(1)} %copy-done.10), custom_call_target="tpu_custom_call" | custom-call | flops 1000000000 | bytes 4000000 | tf_op jit(solution)/shard_map/first/pallas_call | solution.py:410
  6.6 0.0 copy-start.16
  6.6 4.3 %all-to-all-start = ((f32[8,96,128]{2,1,0:T(8,128)}), f32[8,96,128]{2,1,0:T(8,128)S(1)}, u32[]{:S(2)}, u32[]{:S(2)}) async-start(f32[8,96,128]{2,1,0:T(8,128)} %get-tuple-element.19), calls=%async_computation | async-start | bytes 786432 | tf_op jit(solution)/shard_map/all_to_all | solution.py:426
  10.9 0.0 copy-done.1
  11.0 2.3 %local.2 = (f32[6,56,256]{2,1,0:T(8,128)S(1)}, bf16[512,1024]{1,0:T(8,128)(2,1)S(1)}, bf16[112,192]{1,0:T(8,128)(2,1)S(1)}, f32[56,256]{1,0:T(8,128)S(1)}) custom-call(s32[1]{0:T(128)S(6)} %copy.18.live_ref, f32[6,56,256]{2,1,0:T(8,128)S(1)} %get-tuple-element.18.state_ref.residual_ref, bf16[256,1024]{1,0:T(8,128)(2,1)S(1)} %get-tuple-element.20.traces_ref, ...), custom_call_target="tpu_custom_call" | custom-call | flops 4000000000 | bytes 4000000 | tf_op jit(solution)/shard_map/local/pallas_call | solution.py:434
  13.3 0.0 copy-done.16
  13.3 0.0 copy-start.18
  13.3 1.0 %copy-done.18 = bf16[512,1024]{1,0:T(8,128)(2,1)} copy-done((bf16[512,1024]{1,0:T(8,128)(2,1)}, bf16[512,1024]{1,0:T(8,128)(2,1)S(1)}, u32[]{:S(2)}) %copy-start.18) | copy-done | bytes 1048600
  14.3 0.7 %copy-done.21 = f32[6,56,256]{2,1,0:T(8,128)} copy-done((f32[6,56,256]{2,1,0:T(8,128)}, f32[6,56,256]{2,1,0:T(8,128)S(1)}, u32[]{:S(2)}) %copy-start.21) | copy-done | bytes 344088
  15.0 0.6 copy-done.30
  15.7 0.6 copy-done.33
  16.3 3.6 %all-to-all-done.swapped_ref = f32[8,96,128]{2,1,0:T(8,128)S(1)} async-done(((f32[8,96,128]{2,1,0:T(8,128)}), f32[8,96,128]{2,1,0:T(8,128)S(1)}, u32[]{:S(2)}, u32[]{:S(2)}) %all-to-all-start) | async-done | bytes 393248 | tf_op jit(solution)/shard_map/all_to_all | solution.py:426
  19.9 6.6 %collective-permute-start.1 = (f32[8,32,128]{2,1,0:T(8,128)S(1)}, f32[8,32,128]{2,1,0:T(8,128)S(1)}, u32[]{:S(2)}, u32[]{:S(2)}) collective-permute-start(f32[8,32,128]{2,1,0:T(8,128)S(1)} %get-tuple-element.36), channel_id=1, source_target_pairs={{8,16},{16,8},{24,32},{32,24},{40,48},{48,40},{56,64},{64,56},{72,... | collective-permute-start | bytes 393224 | tf_op jit(solution)/shard_map/ppermute | solution.py:32
  26.5 1.9 %collective-permute-start = (f32[8,32,128]{2,1,0:T(8,128)S(1)}, f32[8,32,128]{2,1,0:T(8,128)S(1)}, u32[]{:S(2)}, u32[]{:S(2)}) collective-permute-start(f32[8,32,128]{2,1,0:T(8,128)S(1)} %get-tuple-element.37), channel_id=1, source_target_pairs={{0,8},{8,0},{16,24},{24,16},{32,40},{40,32},{48,56},{56,48},{64,72... | collective-permute-start | bytes 393224 | tf_op jit(solution)/shard_map/ppermute | solution.py:32
  28.4 0.0 copy-start.22
  28.4 1.0 %copy-done.22 = f32[6,56,256]{2,1,0:T(8,128)S(1)} copy-done((f32[6,56,256]{2,1,0:T(8,128)S(1)}, f32[6,56,256]{2,1,0:T(8,128)}, u32[]{:S(2)}) %copy-start.22) | copy-done | bytes 344088
  29.4 0.8 %copy-done.31 = bf16[112,192]{1,0:T(8,128)(2,1)S(1)} copy-done((bf16[112,192]{1,0:T(8,128)(2,1)S(1)}, bf16[112,192]{1,0:T(8,128)(2,1)}, u32[]{:S(2)}) %copy-start.31) | copy-done | bytes 43032
  30.2 1.1 %own.2.partial_ref = f32[6,56,256]{2,1,0:T(8,128)S(1)} custom-call(s32[1]{0:T(128)S(6)} %copy.18.live_ref, f32[6,56,256]{2,1,0:T(8,128)S(1)} %copy-done.22, f32[8,96,128]{2,1,0:T(8,128)S(1)} %all-to-all-done.swapped_ref, f32[4,4,256]{2,1,0:T(4,128)S(1)} %copy-done.5, s32[4,256]{1,0:T(4,128)S(1)} %copy-done.7, s32[4,256]{1,0:T(4,128)S(1)} %copy-done.8, ...), custom_call_target="tpu_custom_call" | custom-call | flops 1500000000 | bytes 4000000 | tf_op jit(solution)/shard_map/own/pallas_call | solution.py:458
  31.3 0.0 collective-permute-done.1.other_ref
  31.3 2.0 %collective-permute-done.first_ref = f32[8,32,128]{2,1,0:T(8,128)S(1)} collective-permute-done((f32[8,32,128]{2,1,0:T(8,128)S(1)}, f32[8,32,128]{2,1,0:T(8,128)S(1)}, u32[]{:S(2)}, u32[]{:S(2)}) %collective-permute-start) | collective-permute-done | bytes 131104 | tf_op jit(solution)/shard_map/ppermute | solution.py:32
  33.3 0.0 copy-done.11
  33.3 0.0 copy-done.19
  33.3 2.9 %final.2 = (f32[6,56,256]{2,1,0:T(8,128)S(1)}, f32[6,56,256]{2,1,0:T(8,128)S(1)}, f32[8,96,128]{2,1,0:T(8,128)}, bf16[256,1024]{1,0:T(8,128)(2,1)S(1)}) custom-call(s32[1]{0:T(128)S(6)} %copy.18.live_ref, f32[6,56,256]{2,1,0:T(8,128)S(1)} %copy-done.17, f32[6,56,256]{2,1,0:T(8,128)S(1)} %copy-done.17, f32[6,56,256]{2,1,0:T(8,128)S(1)} %own.2.partial_ref, ...), custom_call_target="tpu_custom_call" | custom-call | flops 3000000000 | bytes 4000000 | tf_op jit(solution)/shard_map/final/pallas_call | solution.py:470
  36.2 0.8 %copy-done.23 = bf16[256,1024]{1,0:T(8,128)(2,1)} copy-done((bf16[256,1024]{1,0:T(8,128)(2,1)}, bf16[256,1024]{1,0:T(8,128)(2,1)S(1)}, u32[]{:S(2)}) %copy-start.23) | copy-done | bytes 524312
  37.1 0.7 %copy-done.25 = f32[6,56,256]{2,1,0:T(8,128)} copy-done((f32[6,56,256]{2,1,0:T(8,128)}, f32[6,56,256]{2,1,0:T(8,128)S(1)}, u32[]{:S(2)}) %copy-start.25) | copy-done | bytes 344088
  37.8 0.7 %copy-done.28 = f32[6,56,256]{2,1,0:T(8,128)} copy-done((f32[6,56,256]{2,1,0:T(8,128)}, f32[6,56,256]{2,1,0:T(8,128)S(1)}, u32[]{:S(2)}) %copy-start.28) | copy-done | bytes 344088
  38.5 3.5 %all-to-all-start.1 = ((f32[8,96,128]{2,1,0:T(8,128)}), f32[8,96,128]{2,1,0:T(8,128)S(1)}, u32[]{:S(2)}, u32[]{:S(2)}) async-start(f32[8,96,128]{2,1,0:T(8,128)} %get-tuple-element.30), calls=%async_computation.1 | async-start | bytes 786432 | tf_op jit(solution)/shard_map/all_to_all | solution.py:426
  42.0 0.0 copy-start.24
  42.0 1.0 %copy-done.24 = bf16[256,1024]{1,0:T(8,128)(2,1)S(1)} copy-done((bf16[256,1024]{1,0:T(8,128)(2,1)S(1)}, bf16[256,1024]{1,0:T(8,128)(2,1)}, u32[]{:S(2)}) %copy-start.24) | copy-done | bytes 524312
  43.0 1.0 %copy-done.26 = f32[6,56,256]{2,1,0:T(8,128)S(1)} copy-done((f32[6,56,256]{2,1,0:T(8,128)S(1)}, f32[6,56,256]{2,1,0:T(8,128)}, u32[]{:S(2)}) %copy-start.26) | copy-done | bytes 344088
  44.0 2.1 %local.3.partial_ref = f32[6,56,256]{2,1,0:T(8,128)S(1)} custom-call(s32[1]{0:T(128)S(6)} %copy.18.live_ref, f32[6,56,256]{2,1,0:T(8,128)S(1)} %copy-done.26, bf16[256,1024]{1,0:T(8,128)(2,1)S(1)} %copy-done.24, f32[9,256]{1,0:T(8,128)S(1)} %copy-done.4, f32[4,4,256]{2,1,0:T(4,128)S(1)} %copy-done.5, s32[4,256]{1,0:T(4,128)S(1)} %copy-done.7, ...), custom_call_target="tpu_custom_call" | custom-call | flops 4000000000 | bytes 4000000 | tf_op jit(solution)/shard_map/local/pallas_call | solution.py:434
  46.1 4.7 %all-to-all-done.1.swapped_ref = f32[8,96,128]{2,1,0:T(8,128)S(1)} async-done(((f32[8,96,128]{2,1,0:T(8,128)}), f32[8,96,128]{2,1,0:T(8,128)S(1)}, u32[]{:S(2)}, u32[]{:S(2)}) %all-to-all-start.1) | async-done | bytes 393248 | tf_op jit(solution)/shard_map/all_to_all | solution.py:426
  50.9 3.4 %collective-permute-start.3 = (f32[8,32,128]{2,1,0:T(8,128)S(1)}, f32[8,32,128]{2,1,0:T(8,128)S(1)}, u32[]{:S(2)}, u32[]{:S(2)}) collective-permute-start(f32[8,32,128]{2,1,0:T(8,128)S(1)} %get-tuple-element.34), channel_id=1, source_target_pairs={{8,16},{16,8},{24,32},{32,24},{40,48},{48,40},{56,64},{64,56},{72,... | collective-permute-start | bytes 393224 | tf_op jit(solution)/shard_map/ppermute | solution.py:32
  54.3 0.0 copy-start.20
  54.3 0.0 copy-start.27
  54.3 0.0 copy-start.29
  54.3 2.1 %collective-permute-start.2 = (f32[8,32,128]{2,1,0:T(8,128)S(1)}, f32[8,32,128]{2,1,0:T(8,128)S(1)}, u32[]{:S(2)}, u32[]{:S(2)}) collective-permute-start(f32[8,32,128]{2,1,0:T(8,128)S(1)} %get-tuple-element.35), channel_id=1, source_target_pairs={{0,8},{8,0},{16,24},{24,16},{32,40},{40,32},{48,56},{56,48},{64,72... | collective-permute-start | bytes 393224 | tf_op jit(solution)/shard_map/ppermute | solution.py:32
  56.4 1.1 %own.3.partial_ref = f32[6,56,256]{2,1,0:T(8,128)S(1)} custom-call(s32[1]{0:T(128)S(6)} %copy.18.live_ref, f32[6,56,256]{2,1,0:T(8,128)S(1)} %local.3.partial_ref, f32[8,96,128]{2,1,0:T(8,128)S(1)} %all-to-all-done.1.swapped_ref, f32[4,4,256]{2,1,0:T(4,128)S(1)} %copy-done.5, s32[4,256]{1,0:T(4,128)S(1)} %copy-done.7, s32[4,256]{1,0:T(4,128)S(1)} %copy-done.8, ...), custom_call_target="tpu_custom_call" | custom-call | flops 1500000000 | bytes 4000000 | tf_op jit(solution)/shard_map/own/pallas_call | solution.py:458
  57.5 3.6 %collective-permute-done.3.other_ref = f32[8,32,128]{2,1,0:T(8,128)S(1)} collective-permute-done((f32[8,32,128]{2,1,0:T(8,128)S(1)}, f32[8,32,128]{2,1,0:T(8,128)S(1)}, u32[]{:S(2)}, u32[]{:S(2)}) %collective-permute-start.3) | collective-permute-done | bytes 131104 | tf_op jit(solution)/shard_map/ppermute | solution.py:32
  61.1 0.2 collective-permute-done.2.first_ref
  61.3 2.1 %final.3 = (f32[6,56,256]{2,1,0:T(8,128)}, f32[6,56,256]{2,1,0:T(8,128)}) custom-call(s32[1]{0:T(128)S(6)} %copy.18.live_ref, f32[6,56,256]{2,1,0:T(8,128)S(1)} %copy-done.27, f32[6,56,256]{2,1,0:T(8,128)S(1)} %copy-done.29, f32[6,56,256]{2,1,0:T(8,128)S(1)} %own.3.partial_ref, f32[8,32,128]{2,1,0:T(8,128)S(1)} %collective-permute-done.2.first_ref, ...), custom_call_target="tpu_custom_call" | custom-call | flops 3000000000 | bytes 4000000 | tf_op jit(solution)/shard_map/final/pallas_call | solution.py:470
  (43 shorter events, 0.1 us)
Async XLA Ops:
  1.3 1.0 %copy-start = (f32[6,56,256]{2,1,0:T(8,128)S(1)}, f32[6,56,256]{2,1,0:T(8,128)}, u32[]{:S(2)}) copy-start(f32[6,56,256]{2,1,0:T(8,128)} %fields_hbm.1) | copy-start | bytes 1032196
  2.3 0.7 %copy-start.6 = (s32[1,3,8,32]{3,2,1,0:T(8,128)S(1)}, s32[1,3,8,32]{3,2,1,0:T(8,128)}, u32[]{:S(2)}) copy-start(s32[1,3,8,32]{3,2,1,0:T(8,128)} %param.24) | copy-start | bytes 9220
  3.0 1.0 %copy-start.10 = (bf16[512,336]{1,0:T(8,128)(2,1)S(1)}, bf16[512,336]{1,0:T(8,128)(2,1)}, u32[]{:S(2)}) copy-start(bf16[512,336]{1,0:T(8,128)(2,1)} %constant.10.clone.pick_hbm.pick_ref) | copy-start | bytes 1032196
  4.0 6.9 %copy-start.1 = (f32[3,56,56]{2,1,0:T(8,128)S(1)}, f32[3,56,56]{2,1,0:T(8,128)}, u32[]{:S(2)}) copy-start(f32[3,56,56]{2,1,0:T(8,128)} %derivatives_ref.3) | copy-start | bytes 112900
  4.0 7.0 %copy-start.2 = (f32[56,256]{1,0:T(8,128)S(1)}, f32[56,256]{1,0:T(8,128)}, u32[]{:S(2)}) copy-start(f32[56,256]{1,0:T(8,128)} %ratio_ref.3) | copy-start | bytes 172036
  4.0 7.0 %copy-start.3 = (f32[56,84]{1,0:T(8,128)S(1)}, f32[56,84]{1,0:T(8,128)}, u32[]{:S(2)}) copy-start(f32[56,84]{1,0:T(8,128)} %lift_ref.3) | copy-start | bytes 56452
  4.0 7.0 %copy-start.4 = (f32[9,256]{1,0:T(8,128)S(1)}, f32[9,256]{1,0:T(8,128)}, u32[]{:S(2)}) copy-start(f32[9,256]{1,0:T(8,128)} %metric_ref.3) | copy-start | bytes 27652
  4.0 7.0 %copy-start.5 = (f32[4,4,256]{2,1,0:T(4,128)S(1)}, f32[4,4,256]{2,1,0:T(4,128)}, u32[]{:S(2)}) copy-start(f32[4,4,256]{2,1,0:T(4,128)} %geom_ref.11) | copy-start | bytes 49156
  4.0 7.0 %copy-start.7 = (s32[4,256]{1,0:T(4,128)S(1)}, s32[4,256]{1,0:T(4,128)}, u32[]{:S(2)}) copy-start(s32[4,256]{1,0:T(4,128)} %source_ref.7) | copy-start | bytes 12292
  4.0 7.0 %copy-start.8 = (s32[4,256]{1,0:T(4,128)S(1)}, s32[4,256]{1,0:T(4,128)}, u32[]{:S(2)}) copy-start(s32[4,256]{1,0:T(4,128)} %permutation_ref.11) | copy-start | bytes 12292
  4.0 7.0 %copy-start.9 = (s32[256]{0:T(256)S(1)}, s32[256]{0:T(256)}, u32[]{:S(2)}) copy-start(s32[256]{0:T(256)} %param.20) | copy-start | bytes 3076
  4.0 7.0 %copy-start.12 = (bf16[432,144]{1,0:T(8,128)(2,1)S(1)}, bf16[432,144]{1,0:T(8,128)(2,1)}, u32[]{:S(2)}) copy-start(bf16[432,144]{1,0:T(8,128)(2,1)} %constant.12.clone.turn_ref) | copy-start | bytes 373252
  4.0 7.0 %copy-start.13 = (bf16[2,84,192]{2,1,0:T(8,128)(2,1)S(1)}, bf16[2,84,192]{2,1,0:T(8,128)(2,1)}, u32[]{:S(2)}) copy-start(bf16[2,84,192]{2,1,0:T(8,128)(2,1)} %constant.13.clone.spread_lift_ref) | copy-start | bytes 193540
  4.0 7.0 %copy-start.14 = (bf16[144,256]{1,0:T(8,128)(2,1)S(1)}, bf16[144,256]{1,0:T(8,128)(2,1)}, u32[]{:S(2)}) copy-start(bf16[144,256]{1,0:T(8,128)(2,1)} %constant.11.clone.pad_ref) | copy-start | bytes 221188
  4.1 7.0 %copy-start.15 = (bf16[2,56,112]{2,1,0:T(8,128)(2,1)S(1)}, bf16[2,56,112]{2,1,0:T(8,128)(2,1)}, u32[]{:S(2)}) copy-start(bf16[2,56,112]{2,1,0:T(8,128)(2,1)} %constant.14.clone.spread_node_ref) | copy-start | bytes 75268
  6.6 6.7 %copy-start.16 = (f32[6,56,256]{2,1,0:T(8,128)}, f32[6,56,256]{2,1,0:T(8,128)S(1)}, u32[]{:S(2)}) copy-start(f32[6,56,256]{2,1,0:T(8,128)S(1)} %get-tuple-element.18.state_ref.residual_ref) | copy-start | bytes 1032196
  6.6 13.3 %all-to-all-start = ((f32[8,96,128]{2,1,0:T(8,128)}), f32[8,96,128]{2,1,0:T(8,128)S(1)}, u32[]{:S(2)}, u32[]{:S(2)}) async-start(f32[8,96,128]{2,1,0:T(8,128)} %get-tuple-element.19), calls=%async_computation | async-start | bytes 786432 | tf_op jit(solution)/shard_map/all_to_all | solution.py:426
  13.3 1.0 %copy-start.18 = (bf16[512,1024]{1,0:T(8,128)(2,1)}, bf16[512,1024]{1,0:T(8,128)(2,1)S(1)}, u32[]{:S(2)}) copy-start(bf16[512,1024]{1,0:T(8,128)(2,1)S(1)} %get-tuple-element.25.choice_ref) | copy-start | bytes 3145732
  14.3 0.7 %copy-start.21 = (f32[6,56,256]{2,1,0:T(8,128)}, f32[6,56,256]{2,1,0:T(8,128)S(1)}, u32[]{:S(2)}) copy-start(f32[6,56,256]{2,1,0:T(8,128)S(1)} %get-tuple-element.22.partial_ref) | copy-start | bytes 1032196
  15.0 0.6 copy-start.30
  15.7 0.6 copy-start.33
  19.9 11.4 %collective-permute-start.1 = (f32[8,32,128]{2,1,0:T(8,128)S(1)}, f32[8,32,128]{2,1,0:T(8,128)S(1)}, u32[]{:S(2)}, u32[]{:S(2)}) collective-permute-start(f32[8,32,128]{2,1,0:T(8,128)S(1)} %get-tuple-element.36), channel_id=1, source_target_pairs={{8,16},{16,8},{24,32},{32,24},{40,48},{48,40},{56,64},{64,56},{72,... | collective-permute-start | bytes 393224 | tf_op jit(solution)/shard_map/ppermute | solution.py:32
  26.5 6.9 %collective-permute-start = (f32[8,32,128]{2,1,0:T(8,128)S(1)}, f32[8,32,128]{2,1,0:T(8,128)S(1)}, u32[]{:S(2)}, u32[]{:S(2)}) collective-permute-start(f32[8,32,128]{2,1,0:T(8,128)S(1)} %get-tuple-element.37), channel_id=1, source_target_pairs={{0,8},{8,0},{16,24},{24,16},{32,40},{40,32},{48,56},{56,48},{64,72... | collective-permute-start | bytes 393224 | tf_op jit(solution)/shard_map/ppermute | solution.py:32
  28.4 1.0 %copy-start.22 = (f32[6,56,256]{2,1,0:T(8,128)S(1)}, f32[6,56,256]{2,1,0:T(8,128)}, u32[]{:S(2)}) copy-start(f32[6,56,256]{2,1,0:T(8,128)} %copy-done.21) | copy-start | bytes 1032196
  29.4 0.8 %copy-start.31 = (bf16[112,192]{1,0:T(8,128)(2,1)S(1)}, bf16[112,192]{1,0:T(8,128)(2,1)}, u32[]{:S(2)}) copy-start(bf16[112,192]{1,0:T(8,128)(2,1)} %copy-done.30) | copy-start | bytes 129028
  30.2 3.1 %copy-start.11 = (bf16[512,336]{1,0:T(8,128)(2,1)S(1)}, bf16[512,336]{1,0:T(8,128)(2,1)}, u32[]{:S(2)}) copy-start(bf16[512,336]{1,0:T(8,128)(2,1)} %constant.10.clone.pick_hbm.pick_ref) | copy-start | bytes 1032196
  30.2 3.1 %copy-start.17 = (f32[6,56,256]{2,1,0:T(8,128)S(1)}, f32[6,56,256]{2,1,0:T(8,128)}, u32[]{:S(2)}) copy-start(f32[6,56,256]{2,1,0:T(8,128)} %copy-done.16) | copy-start | bytes 1032196
  30.2 3.1 %copy-start.19 = (bf16[512,1024]{1,0:T(8,128)(2,1)S(1)}, bf16[512,1024]{1,0:T(8,128)(2,1)}, u32[]{:S(2)}) copy-start(bf16[512,1024]{1,0:T(8,128)(2,1)} %copy-done.18) | copy-start | bytes 3145732
  30.2 3.1 %copy-start.34 = (f32[56,256]{1,0:T(8,128)S(1)}, f32[56,256]{1,0:T(8,128)}, u32[]{:S(2)}) copy-start(f32[56,256]{1,0:T(8,128)} %copy-done.33) | copy-start | bytes 172036
  36.2 0.8 %copy-start.23 = (bf16[256,1024]{1,0:T(8,128)(2,1)}, bf16[256,1024]{1,0:T(8,128)(2,1)S(1)}, u32[]{:S(2)}) copy-start(bf16[256,1024]{1,0:T(8,128)(2,1)S(1)} %get-tuple-element.31.traces_ref) | copy-start | bytes 1572868
  37.1 0.7 %copy-start.25 = (f32[6,56,256]{2,1,0:T(8,128)}, f32[6,56,256]{2,1,0:T(8,128)S(1)}, u32[]{:S(2)}) copy-start(f32[6,56,256]{2,1,0:T(8,128)S(1)} %get-tuple-element.28.state_ref) | copy-start | bytes 1032196
  37.8 0.7 %copy-start.28 = (f32[6,56,256]{2,1,0:T(8,128)}, f32[6,56,256]{2,1,0:T(8,128)S(1)}, u32[]{:S(2)}) copy-start(f32[6,56,256]{2,1,0:T(8,128)S(1)} %get-tuple-element.29.residual_ref) | copy-start | bytes 1032196
  38.5 12.3 %all-to-all-start.1 = ((f32[8,96,128]{2,1,0:T(8,128)}), f32[8,96,128]{2,1,0:T(8,128)S(1)}, u32[]{:S(2)}, u32[]{:S(2)}) async-start(f32[8,96,128]{2,1,0:T(8,128)} %get-tuple-element.30), calls=%async_computation.1 | async-start | bytes 786432 | tf_op jit(solution)/shard_map/all_to_all | solution.py:426
  42.0 1.0 %copy-start.24 = (bf16[256,1024]{1,0:T(8,128)(2,1)S(1)}, bf16[256,1024]{1,0:T(8,128)(2,1)}, u32[]{:S(2)}) copy-start(bf16[256,1024]{1,0:T(8,128)(2,1)} %copy-done.23) | copy-start | bytes 1572868
  43.0 1.0 %copy-start.26 = (f32[6,56,256]{2,1,0:T(8,128)S(1)}, f32[6,56,256]{2,1,0:T(8,128)}, u32[]{:S(2)}) copy-start(f32[6,56,256]{2,1,0:T(8,128)} %copy-done.25) | copy-start | bytes 1032196
  44.0 12.4 %copy-start.32 = (bf16[112,192]{1,0:T(8,128)(2,1)S(1)}, bf16[112,192]{1,0:T(8,128)(2,1)}, u32[]{:S(2)}) copy-start(bf16[112,192]{1,0:T(8,128)(2,1)} %copy-done.30) | copy-start | bytes 129028
  50.9 10.3 %collective-permute-start.3 = (f32[8,32,128]{2,1,0:T(8,128)S(1)}, f32[8,32,128]{2,1,0:T(8,128)S(1)}, u32[]{:S(2)}, u32[]{:S(2)}) collective-permute-start(f32[8,32,128]{2,1,0:T(8,128)S(1)} %get-tuple-element.34), channel_id=1, source_target_pairs={{8,16},{16,8},{24,32},{32,24},{40,48},{48,40},{56,64},{64,56},{72,... | collective-permute-start | bytes 393224 | tf_op jit(solution)/shard_map/ppermute | solution.py:32
  54.3 7.0 %copy-start.20 = (bf16[512,1024]{1,0:T(8,128)(2,1)S(1)}, bf16[512,1024]{1,0:T(8,128)(2,1)}, u32[]{:S(2)}) copy-start(bf16[512,1024]{1,0:T(8,128)(2,1)} %copy-done.18) | copy-start | bytes 3145732
  54.3 7.0 %copy-start.27 = (f32[6,56,256]{2,1,0:T(8,128)S(1)}, f32[6,56,256]{2,1,0:T(8,128)}, u32[]{:S(2)}) copy-start(f32[6,56,256]{2,1,0:T(8,128)} %copy-done.25) | copy-start | bytes 1032196
  54.3 7.0 %copy-start.29 = (f32[6,56,256]{2,1,0:T(8,128)S(1)}, f32[6,56,256]{2,1,0:T(8,128)}, u32[]{:S(2)}) copy-start(f32[6,56,256]{2,1,0:T(8,128)} %copy-done.28) | copy-start | bytes 1032196
  54.3 7.0 %collective-permute-start.2 = (f32[8,32,128]{2,1,0:T(8,128)S(1)}, f32[8,32,128]{2,1,0:T(8,128)S(1)}, u32[]{:S(2)}, u32[]{:S(2)}) collective-permute-start(f32[8,32,128]{2,1,0:T(8,128)S(1)} %get-tuple-element.35), channel_id=1, source_target_pairs={{0,8},{8,0},{16,24},{24,16},{32,40},{40,32},{48,56},{56,48},{64,72... | collective-permute-start | bytes 393224 | tf_op jit(solution)/shard_map/ppermute | solution.py:32

commit v3 on v2

--- a/solution.py
+++ b/solution.py
@@ -198,9 +198,9 @@
     send_hbm,
     pick_hbm,
     out_ref,
-    choice_ref,
     state_ref,
     traces_ref,
+    choice_ref,
     fields_ref,
     send_ref,
     pick_ref,
@@ -225,7 +225,6 @@
 
 
 def local_kernel(
-    step,
     live_ref,
     state_ref,
     traces_ref,
@@ -239,20 +238,23 @@
     turn_ref,
     spread_lift_ref,
     spread_node_ref,
-    ratio_ref,
-    curved_ref,
+    swapped_ref,
     out_ref,
-    *prepared,
 ):
     elements = state_ref.shape[2]
+    slots = swapped_ref.shape[1] // 3
+    own = high_over_low(swapped_ref[:, slots : 2 * slots].reshape(-1, PACKED))
+    own_base = 4 * elements + own.shape[1]
     n, half = normals(geom_ref)
     source, permutation = row_of_faces(source_ref), row_of_faces(permutation_ref)
     lift = stacked_weights(lift_ref[...], spread_lift_ref)
     traces = traces_ref[...]
     gathered = []
     for f in range(4):
-        chosen = one_hot(source_ref[f : f + 1], 4 * elements, 0)
-        gathered.append(mm(traces, chosen).astype(BF16))
+        source_row = source_ref[f : f + 1]
+        near = mm(traces, one_hot(source_row, 4 * elements, 0))
+        far = mm(own, one_hot(source_row, own.shape[1], own_base))
+        gathered.append((near + far).astype(BF16))
     gathered = jnp.concatenate(gathered, axis=1)
     flux = turned(flux_h(mm(pad_ref[...], gathered), n, half), permutation, turn_ref[...])
     flux = flux - flux_h(mm(pad_ref[...], traces), n, half)
@@ -276,53 +278,33 @@
         rate[base + second] = rate[base + second] - sign * gradient(first)
     for c in range(6):
         out_ref[c] = rate[c]
-    if step == 0:
-        choice_ref, lift_out_ref, scaling_ref = prepared
-        lift_out_ref[...] = lift
-        ratio = jnp.where(curved_ref[...] == 1, ratio_ref[...], 1.0)
-        scaling_ref[...] = ratio * alive(live_ref, elements)
-        even = even_group()
-        block = choice_ref.shape[0] // 2
-        start = 4 * elements
-        near, far = start, start + 2 * block
-        first_base = jnp.where(even, near, far)
-        other_base = jnp.where(even, far, near)
-        choice_ref[:block] = one_hot(source, block, first_base)
-        choice_ref[block:] = one_hot(source, block, other_base)
+
+
+def partner_choice(source, slots):
+    even = even_group()
+    near = source.shape[1]
+    far = near + 2 * slots
+    bases = [jnp.where(even, near, far), jnp.where(even, far, near)]
+    return jnp.concatenate([one_hot(source, slots, base) for base in bases], axis=0)
+
+
+def high_over_low(table):
+    high, low = halves(jnp.transpose(table, (1, 0)))
+    return jnp.concatenate([high, low], axis=0)
 
 
 def received_flux(tables, choice, geom_ref, permutation_ref, pad_ref, turn_ref):
-    columns = []
-    for table in tables:
-        high, low = halves(jnp.transpose(table, (1, 0)))
-        columns.append(jnp.concatenate([high, low], axis=0))
+    columns = [high_over_low(table) for table in tables]
     n, half = normals(geom_ref)
     gathered = mm(jnp.concatenate(columns, axis=1), choice).astype(BF16)
     flux = flux_h(mm(pad_ref[...], gathered), n, half)
     return turned(flux, row_of_faces(permutation_ref), turn_ref[...]), n
 
 
-def own_kernel(
-    live_ref,
-    partial_ref,
-    swapped_ref,
-    geom_ref,
-    source_ref,
-    permutation_ref,
-    lift_ref,
-    pad_ref,
-    turn_ref,
-    out_ref,
-):
-    slots = swapped_ref.shape[1] // 3
-    table = swapped_ref[:, slots : 2 * slots].reshape(-1, PACKED)
-    count = table.shape[0]
-    base = 4 * source_ref.shape[1] + count
-    choice = one_hot(row_of_faces(source_ref), count, base)
-    flux, n = received_flux([table], choice, geom_ref, permutation_ref, pad_ref, turn_ref)
-    lifted = lifted_from(flux, n, lift_ref[...])
-    for c in range(6):
-        out_ref[c] = partial_ref[c] + lifted[c]
+def split_kernel(live_ref, swapped_ref, first_ref, other_ref):
+    slots = first_ref.shape[1]
+    first_ref[...] = swapped_ref[:, :slots]
+    other_ref[...] = swapped_ref[:, 2 * slots :]
 
 
 def final_kernel(
@@ -333,23 +315,25 @@
     partial_ref,
     first_ref,
     other_ref,
-    choice_ref,
+    source_ref,
     geom_ref,
     permutation_ref,
-    scaling_ref,
+    ratio_ref,
+    curved_ref,
     lift_ref,
     pad_ref,
     turn_ref,
+    spread_lift_ref,
     pick_ref,
-    outgoing_choice_ref,
+    send_ref,
     *out_refs,
 ):
     tables = [r[...].reshape(-1, PACKED) for r in (first_ref, other_ref)]
-    flux, n = received_flux(
-        tables, choice_ref[...], geom_ref, permutation_ref, pad_ref, turn_ref
-    )
-    lifted = lifted_from(flux, n, lift_ref[...])
-    scaling = scaling_ref[...]
+    choice = partner_choice(row_of_faces(source_ref), tables[0].shape[0])
+    flux, n = received_flux(tables, choice, geom_ref, permutation_ref, pad_ref, turn_ref)
+    lifted = lifted_from(flux, n, stacked_weights(lift_ref[...], spread_lift_ref))
+    scaling = jnp.where(curved_ref[...] == 1, ratio_ref[...], 1.0)
+    scaling = scaling * alive(live_ref, scaling.shape[1])
     state_out, residual_out = out_refs[:2]
     advanced = []
     for c in range(6):
@@ -363,7 +347,7 @@
     if step == 0:
         traces = traces_of(jnp.concatenate(advanced, axis=0), pick_ref[...])
         out_refs[3][...] = traces
-        pack(outgoing_choice_ref[...], traces, out_refs[2])
+        pack(outgoing_choice(send_ref[...], traces.shape[1]), traces, out_refs[2])
 
 
 VMEM = pl.BlockSpec(memory_space=pltpu.VMEM)
@@ -378,7 +362,7 @@
         in_specs=[SMEM] + [space] * count,
         out_specs=jax.tree.map(lambda _: VMEM, out_shape),
         scratch_shapes=scratch,
-        compiler_params=pltpu.CompilerParams(vmem_limit_bytes=40 * 1024 * 1024),
+        compiler_params=pltpu.CompilerParams(vmem_limit_bytes=24 * 1024 * 1024),
         cost_estimate=pl.CostEstimate(flops=flops, bytes_accessed=4_000_000, transcendentals=0),
         name=name,
     )
@@ -407,33 +391,30 @@
     outgoing_shape = shape((8, 3 * slots, PACKED), F32)
     traces_shape = shape((2 * PACKED, 4 * elements), BF16)
 
-    outgoing, outgoing_rows, current, traces = call(
+    outgoing, current, traces = call(
         first_kernel,
         HBM,
         3,
-        [outgoing_shape, shape((24 * slots, 4 * elements), BF16), whole, traces_shape],
+        [outgoing_shape, whole, traces_shape],
         "first",
         1_000_000_000,
         scratch=[
+            pltpu.VMEM((24 * slots, 4 * elements), BF16),
             pltpu.VMEM(fields.shape, F32),
             pltpu.VMEM(send.shape, jnp.int32),
             pltpu.VMEM(pick.shape, BF16),
             pltpu.SemaphoreType.DMA((3,)),
         ],
-    )(live_count, fields, send, pick)
+    )(live_count, *(pltpu.with_memory_space_constraint(x, pltpu.HBM) for x in (fields, send, pick)))
     residual = current
     for step in range(2):
         swapped = lax.all_to_all(outgoing, "sub", split_axis=0, concat_axis=0, tiled=True)
-        shapes = [whole]
-        if step == 0:
-            shapes += [
-                shape((16 * slots, 4 * elements), BF16),
-                shape((2 * NODES, 8 * PADDED), BF16),
-                shape((NODES, elements), F32),
-            ]
-        partial, *prepared = call(
-            functools.partial(local_kernel, step), VMEM, 14, shapes, "local", 4_000_000_000
-        )(
+        first, other = call(
+            split_kernel, VMEM, 1, [shape((8, slots, PACKED), F32)] * 2, "split", 1_000_000
+        )(live_count, swapped)
+        first = swapped_pairs(first, "dom", 0)
+        other = swapped_pairs(other, "dom", 1)
+        partial = call(local_kernel, VMEM, 13, whole, "local", 4_000_000_000)(
             live_count,
             current,
             traces,
@@ -447,28 +428,11 @@
             turn,
             spread_lift,
             spread_node,
-            jacobian_ratio,
-            curved_row,
-        )
-        if step == 0:
-            choice, lift, scaling = prepared
-        swapped, partial = lax.optimization_barrier((swapped, partial))
-        first = swapped_pairs(swapped[:, :slots], "dom", 0)
-        other = swapped_pairs(swapped[:, 2 * slots :], "dom", 1)
-        partial = call(own_kernel, VMEM, 8, whole, "own", 1_500_000_000)(
-            live_count,
-            partial,
             swapped,
-            face_geom,
-            face_source,
-            face_permutation,
-            lift,
-            pad,
-            turn,
         )
         shapes = [whole, whole] + ([outgoing_shape, traces_shape] if step == 0 else [])
         current, residual, *rest = call(
-            functools.partial(final_kernel, step), VMEM, 14, shapes, "final", 3_000_000_000
+            functools.partial(final_kernel, step), VMEM, 16, shapes, "final", 3_000_000_000
         )(
             live_count,
             current,
@@ -476,15 +440,17 @@
             partial,
             first,
             other,
-            choice,
+            face_source,
             face_geom,
             face_permutation,
-            scaling,
-            lift,
+            jacobian_ratio,
+            curved_row,
+            lift_matrix,
             pad,
             turn,
+            spread_lift,
             pick,
-            outgoing_rows,
+            send,
         )
         if rest:
             outgoing, traces = rest

time: 64.1 us -> 58.8 us (0.917)
  the two profiles are of different devices: /device:TPU:384 before, /device:TPU:256 now
where the time goes in v3:
time: 58.8 us; the launch traced here: 58.4 us
  blocking collectives  24.5 us (42%)
  starting transfers between devices  12.8 us (22%)
  Pallas kernels  11.1 us (19%)
  waiting for transfers between devices  8.41 us (14%)
  between operations  1.54 us (3%)
    all_to_all x2, blocking collectives, on_device(): lax.all_to_all(outgoing, 'sub', split_axis=0, concat_axis=0, tiled=True)  24.5 us
    ppermute x4, starting transfers between devices, swapped_pairs(): return lax.ppermute(array, axis, pairs)  12.8 us
    ppermute x4, waiting for transfers between devices, swapped_pairs(): return lax.ppermute(array, axis, pairs)  8.41 us
    pallas_call x2, Pallas kernels, on_device(): call(local_kernel, VMEM, 13, whole, 'local', 4000000000)  4.57 us
    pallas_call x2, Pallas kernels, on_device(): call(functools.partial(final_kernel, step), VMEM, 16, shapes, 'final', 30...  4.26 us
    pallas_call x1, Pallas kernels, on_device(): call(first_kernel, HBM, 3, [outgoing_shape, whole, traces_shape], 'first'...  2.23 us
  transfers between devices with their start and end apart: 4, of which 2 were waited for; matrix products, arithmetic and copies ran while one was open for 0% of the time, Pallas kernels for 8%

profile of v3, /device:TPU:256, one launch (start us, length us, event | category | flops | bytes accessed | tf_op | source)
XLA Modules:
  0.0 58.4 jit_solution(11935370737219133723)
XLA Ops:
  1.3 2.2 %first.1 = (f32[8,96,128]{2,1,0:T(8,128)S(1)}, f32[6,56,256]{2,1,0:T(8,128)S(1)}, bf16[256,1024]{1,0:T(8,128)(2,1)S(1)}) custom-call(s32[1]{0:T(128)S(6)} %copy.18.live_ref, f32[6,56,256]{2,1,0:T(8,128)} %fields_hbm.1, s32[24,32]{1,0:T(8,128)} %bitcast.2, bf16[512,336]{1,0:T(8,128)(2,1)} %constant.10.clone.pick_hbm.pick_ref), custom_call_target="tpu_custom_call" | custom-call | flops 1000000000 | bytes 4000000 | tf_op jit(solution)/shard_map/first/pallas_call | solution.py:394
  3.5 0.0 copy-start.11
  3.5 0.0 copy-start.12
  3.5 0.0 copy-start.13
  3.6 13.2 %all_to_all.10.swapped_ref = f32[8,96,128]{2,1,0:T(8,128)S(1)} all-to-all(f32[8,96,128]{2,1,0:T(8,128)S(1)} %get-tuple-element.15), channel_id=1, replica_groups=mesh['dom'=64,'sub'=8] {'sub'}, dimensions={0} | all-to-all | bytes 786432 | tf_op jit(solution)/shard_map/all_to_all | solution.py:411
  16.7 0.0 copy-start
  16.7 0.0 copy-start.2
  16.7 0.0 copy-start.3
  16.7 0.0 copy-start.4
  16.7 0.0 copy-start.7
  16.8 0.0 copy-start.10
  16.8 0.0 copy-start.6
  16.8 3.6 %collective-permute-start = (f32[8,32,128]{2,1,0:T(8,128)S(1)}, f32[8,32,128]{2,1,0:T(8,128)S(1)}, u32[]{:S(2)}, u32[]{:S(2)}) collective-permute-start(f32[8,32,128]{2,1,0:T(8,128)S(1)} %get-tuple-element.16), channel_id=1, source_target_pairs={{0,8},{8,0},{16,24},{24,16},{32,40},{40,32},{48,56},{56,48},{64,72... | collective-permute-start | bytes 393224 | tf_op jit(solution)/shard_map/ppermute | solution.py:32
  20.4 3.6 %collective-permute-start.1 = (f32[8,32,128]{2,1,0:T(8,128)S(1)}, f32[8,32,128]{2,1,0:T(8,128)S(1)}, u32[]{:S(2)}, u32[]{:S(2)}) collective-permute-start(f32[8,32,128]{2,1,0:T(8,128)S(1)} %get-tuple-element.17), channel_id=1, source_target_pairs={{8,16},{16,8},{24,32},{32,24},{40,48},{48,40},{56,64},{64,56},{72,... | collective-permute-start | bytes 393224 | tf_op jit(solution)/shard_map/ppermute | solution.py:32
  24.1 0.0 copy-done.11
  24.1 0.0 copy-done.12
  24.1 0.0 copy-done.13
  24.1 0.0 copy-done
  24.1 0.0 copy-done.2
  24.1 0.0 copy-done.3
  24.1 0.0 copy-done.4
  24.1 0.0 copy-done.7
  24.2 0.0 copy-done.10
  24.2 0.0 copy-done.6
  24.2 0.0 copy-start.1
  24.2 0.0 copy-start.5
  24.2 0.0 copy-start.9
  24.2 2.3 %local.2.partial_ref = f32[6,56,256]{2,1,0:T(8,128)S(1)} custom-call(s32[1]{0:T(128)S(6)} %copy.18.live_ref, f32[6,56,256]{2,1,0:T(8,128)S(1)} %get-tuple-element.13.state_ref.residual_ref, bf16[256,1024]{1,0:T(8,128)(2,1)S(1)} %get-tuple-element.14.traces_ref, f32[9,256]{1,0:T(8,128)S(1)} %copy-done.3, f32[4,4,256]{2,1,0:T(4,128)S(1)} %copy-done.4, ...), custom_call_target="tpu_custom_call" | custom-call | flops 4000000000 | bytes 4000000 | tf_op jit(solution)/shard_map/local/pallas_call | solution.py:417
  26.5 0.0 copy-start.8
  26.5 0.0 collective-permute-done.first_ref
  26.5 4.1 %collective-permute-done.1.other_ref = f32[8,32,128]{2,1,0:T(8,128)S(1)} collective-permute-done((f32[8,32,128]{2,1,0:T(8,128)S(1)}, f32[8,32,128]{2,1,0:T(8,128)S(1)}, u32[]{:S(2)}, u32[]{:S(2)}) %collective-permute-start.1) | collective-permute-done | bytes 131104 | tf_op jit(solution)/shard_map/ppermute | solution.py:32
  30.6 0.0 copy-done.1
  30.6 0.0 copy-done.5
  30.6 0.0 copy-done.9
  30.6 0.0 copy-done.8
  30.6 2.2 %final.2 = (f32[6,56,256]{2,1,0:T(8,128)S(1)}, f32[6,56,256]{2,1,0:T(8,128)S(1)}, f32[8,96,128]{2,1,0:T(8,128)S(1)}, bf16[256,1024]{1,0:T(8,128)(2,1)S(1)}) custom-call(s32[1]{0:T(128)S(6)} %copy.18.live_ref, f32[6,56,256]{2,1,0:T(8,128)S(1)} %get-tuple-element.13.state_ref.residual_ref, f32[6,56,256]{2,1,0:T(8,128)S(1)} %get-tuple-element.13.state_ref.residual_ref, ...), custom_call_target="tpu_custom_call" | custom-call | flops 3000000000 | bytes 4000000 | tf_op jit(solution)/shard_map/final/pallas_call | solution.py:434
  32.8 11.3 %all_to_all.11.swapped_ref = f32[8,96,128]{2,1,0:T(8,128)S(1)} all-to-all(f32[8,96,128]{2,1,0:T(8,128)S(1)} %get-tuple-element.21), channel_id=1, replica_groups=mesh['dom'=64,'sub'=8] {'sub'}, dimensions={0} | all-to-all | bytes 786432 | tf_op jit(solution)/shard_map/all_to_all | solution.py:411
  44.2 1.9 %collective-permute-start.2 = (f32[8,32,128]{2,1,0:T(8,128)S(1)}, f32[8,32,128]{2,1,0:T(8,128)S(1)}, u32[]{:S(2)}, u32[]{:S(2)}) collective-permute-start(f32[8,32,128]{2,1,0:T(8,128)S(1)} %get-tuple-element.22), channel_id=1, source_target_pairs={{0,8},{8,0},{16,24},{24,16},{32,40},{40,32},{48,56},{56,48},{64,72... | collective-permute-start | bytes 393224 | tf_op jit(solution)/shard_map/ppermute | solution.py:32
  46.1 3.6 %collective-permute-start.3 = (f32[8,32,128]{2,1,0:T(8,128)S(1)}, f32[8,32,128]{2,1,0:T(8,128)S(1)}, u32[]{:S(2)}, u32[]{:S(2)}) collective-permute-start(f32[8,32,128]{2,1,0:T(8,128)S(1)} %get-tuple-element.23), channel_id=1, source_target_pairs={{8,16},{16,8},{24,32},{32,24},{40,48},{48,40},{56,64},{64,56},{72,... | collective-permute-start | bytes 393224 | tf_op jit(solution)/shard_map/ppermute | solution.py:32
  49.7 2.3 %local.3.partial_ref = f32[6,56,256]{2,1,0:T(8,128)S(1)} custom-call(s32[1]{0:T(128)S(6)} %copy.18.live_ref, f32[6,56,256]{2,1,0:T(8,128)S(1)} %get-tuple-element.18.state_ref, bf16[256,1024]{1,0:T(8,128)(2,1)S(1)} %get-tuple-element.20.traces_ref, f32[9,256]{1,0:T(8,128)S(1)} %copy-done.3, f32[4,4,256]{2,1,0:T(4,128)S(1)} %copy-done.4, ...), custom_call_target="tpu_custom_call" | custom-call | flops 4000000000 | bytes 4000000 | tf_op jit(solution)/shard_map/local/pallas_call | solution.py:417
  52.0 0.0 collective-permute-done.2.first_ref
  52.0 4.3 %collective-permute-done.3.other_ref = f32[8,32,128]{2,1,0:T(8,128)S(1)} collective-permute-done((f32[8,32,128]{2,1,0:T(8,128)S(1)}, f32[8,32,128]{2,1,0:T(8,128)S(1)}, u32[]{:S(2)}, u32[]{:S(2)}) %collective-permute-start.3) | collective-permute-done | bytes 131104 | tf_op jit(solution)/shard_map/ppermute | solution.py:32
  56.4 2.1 %final.3 = (f32[6,56,256]{2,1,0:T(8,128)}, f32[6,56,256]{2,1,0:T(8,128)}) custom-call(s32[1]{0:T(128)S(6)} %copy.18.live_ref, f32[6,56,256]{2,1,0:T(8,128)S(1)} %get-tuple-element.18.state_ref, f32[6,56,256]{2,1,0:T(8,128)S(1)} %get-tuple-element.19.residual_ref, f32[6,56,256]{2,1,0:T(8,128)S(1)} %local.3.partial_ref, ...), custom_call_target="tpu_custom_call" | custom-call | flops 3000000000 | bytes 4000000 | tf_op jit(solution)/shard_map/final/pallas_call | solution.py:434
  (2 shorter events, 0.0 us)
Async XLA Ops:
  3.5 20.6 %copy-start.11 = (bf16[2,84,192]{2,1,0:T(8,128)(2,1)S(1)}, bf16[2,84,192]{2,1,0:T(8,128)(2,1)}, u32[]{:S(2)}) copy-start(bf16[2,84,192]{2,1,0:T(8,128)(2,1)} %constant.13.clone.spread_lift_ref) | copy-start | bytes 193540
  3.5 20.6 %copy-start.12 = (bf16[144,256]{1,0:T(8,128)(2,1)S(1)}, bf16[144,256]{1,0:T(8,128)(2,1)}, u32[]{:S(2)}) copy-start(bf16[144,256]{1,0:T(8,128)(2,1)} %constant.11.clone.pad_ref) | copy-start | bytes 221188
  3.5 20.6 %copy-start.13 = (bf16[2,56,112]{2,1,0:T(8,128)(2,1)S(1)}, bf16[2,56,112]{2,1,0:T(8,128)(2,1)}, u32[]{:S(2)}) copy-start(bf16[2,56,112]{2,1,0:T(8,128)(2,1)} %constant.14.clone.spread_node_ref) | copy-start | bytes 75268
  16.7 7.4 %copy-start = (f32[3,56,56]{2,1,0:T(8,128)S(1)}, f32[3,56,56]{2,1,0:T(8,128)}, u32[]{:S(2)}) copy-start(f32[3,56,56]{2,1,0:T(8,128)} %derivatives_ref.3) | copy-start | bytes 112900
  16.7 7.4 %copy-start.2 = (f32[56,84]{1,0:T(8,128)S(1)}, f32[56,84]{1,0:T(8,128)}, u32[]{:S(2)}) copy-start(f32[56,84]{1,0:T(8,128)} %lift_ref.7) | copy-start | bytes 56452
  16.7 7.4 %copy-start.3 = (f32[9,256]{1,0:T(8,128)S(1)}, f32[9,256]{1,0:T(8,128)}, u32[]{:S(2)}) copy-start(f32[9,256]{1,0:T(8,128)} %metric_ref.3) | copy-start | bytes 27652
  16.7 7.4 %copy-start.4 = (f32[4,4,256]{2,1,0:T(4,128)S(1)}, f32[4,4,256]{2,1,0:T(4,128)}, u32[]{:S(2)}) copy-start(f32[4,4,256]{2,1,0:T(4,128)} %geom_ref.7) | copy-start | bytes 49156
  16.7 7.4 %copy-start.7 = (s32[4,256]{1,0:T(4,128)S(1)}, s32[4,256]{1,0:T(4,128)}, u32[]{:S(2)}) copy-start(s32[4,256]{1,0:T(4,128)} %permutation_ref.7) | copy-start | bytes 12292
  16.8 7.4 %copy-start.10 = (bf16[432,144]{1,0:T(8,128)(2,1)S(1)}, bf16[432,144]{1,0:T(8,128)(2,1)}, u32[]{:S(2)}) copy-start(bf16[432,144]{1,0:T(8,128)(2,1)} %constant.12.clone.turn_ref) | copy-start | bytes 373252
  16.8 7.4 %copy-start.6 = (s32[4,256]{1,0:T(4,128)S(1)}, s32[4,256]{1,0:T(4,128)}, u32[]{:S(2)}) copy-start(s32[4,256]{1,0:T(4,128)} %source_ref.7) | copy-start | bytes 12292
  16.8 9.7 %collective-permute-start = (f32[8,32,128]{2,1,0:T(8,128)S(1)}, f32[8,32,128]{2,1,0:T(8,128)S(1)}, u32[]{:S(2)}, u32[]{:S(2)}) collective-permute-start(f32[8,32,128]{2,1,0:T(8,128)S(1)} %get-tuple-element.16), channel_id=1, source_target_pairs={{0,8},{8,0},{16,24},{24,16},{32,40},{40,32},{48,56},{56,48},{64,72... | collective-permute-start | bytes 393224 | tf_op jit(solution)/shard_map/ppermute | solution.py:32
  20.4 10.2 %collective-permute-start.1 = (f32[8,32,128]{2,1,0:T(8,128)S(1)}, f32[8,32,128]{2,1,0:T(8,128)S(1)}, u32[]{:S(2)}, u32[]{:S(2)}) collective-permute-start(f32[8,32,128]{2,1,0:T(8,128)S(1)} %get-tuple-element.17), channel_id=1, source_target_pairs={{8,16},{16,8},{24,32},{32,24},{40,48},{48,40},{56,64},{64,56},{72,... | collective-permute-start | bytes 393224 | tf_op jit(solution)/shard_map/ppermute | solution.py:32
  24.2 6.4 %copy-start.1 = (f32[56,256]{1,0:T(8,128)S(1)}, f32[56,256]{1,0:T(8,128)}, u32[]{:S(2)}) copy-start(f32[56,256]{1,0:T(8,128)} %ratio_ref.3) | copy-start | bytes 172036
  24.2 6.4 %copy-start.5 = (s32[1,3,8,32]{3,2,1,0:T(8,128)S(1)}, s32[1,3,8,32]{3,2,1,0:T(8,128)}, u32[]{:S(2)}) copy-start(s32[1,3,8,32]{3,2,1,0:T(8,128)} %param.24) | copy-start | bytes 9220
  24.2 6.4 %copy-start.9 = (bf16[512,336]{1,0:T(8,128)(2,1)S(1)}, bf16[512,336]{1,0:T(8,128)(2,1)}, u32[]{:S(2)}) copy-start(bf16[512,336]{1,0:T(8,128)(2,1)} %constant.10.clone.pick_hbm.pick_ref) | copy-start | bytes 1032196
  26.5 4.1 %copy-start.8 = (s32[256]{0:T(256)S(1)}, s32[256]{0:T(256)}, u32[]{:S(2)}) copy-start(s32[256]{0:T(256)} %param.20) | copy-start | bytes 3076
  44.2 7.9 %collective-permute-start.2 = (f32[8,32,128]{2,1,0:T(8,128)S(1)}, f32[8,32,128]{2,1,0:T(8,128)S(1)}, u32[]{:S(2)}, u32[]{:S(2)}) collective-permute-start(f32[8,32,128]{2,1,0:T(8,128)S(1)} %get-tuple-element.22), channel_id=1, source_target_pairs={{0,8},{8,0},{16,24},{24,16},{32,40},{40,32},{48,56},{56,48},{64,72... | collective-permute-start | bytes 393224 | tf_op jit(solution)/shard_map/ppermute | solution.py:32
  46.1 10.3 %collective-permute-start.3 = (f32[8,32,128]{2,1,0:T(8,128)S(1)}, f32[8,32,128]{2,1,0:T(8,128)S(1)}, u32[]{:S(2)}, u32[]{:S(2)}) collective-permute-start(f32[8,32,128]{2,1,0:T(8,128)S(1)} %get-tuple-element.23), channel_id=1, source_target_pairs={{8,16},{16,8},{24,32},{32,24},{40,48},{48,40},{56,64},{64,56},{72,... | collective-permute-start | bytes 393224 | tf_op jit(solution)/shard_map/ppermute | solution.py:32

commit v4 on v3

--- a/solution.py
+++ b/solution.py
@@ -17,7 +17,8 @@
 NODES = 56
 TRACE = 21
 PADDED = 24
-PACKED = 128
+TRIPLE = 64
+PACKED = 2 * TRIPLE
 EXT = 6 * PADDED
 HALF = 3 * PADDED
 F32 = jnp.float32
@@ -58,19 +59,23 @@
 
 def constant_matrices():
     face_nodes, permuted = node_tables()
-    pick = np.zeros((4 * PACKED, 6 * NODES), np.float32)
+    pick = np.zeros((4 * TRIPLE, 3 * NODES), np.float32)
     pad = np.zeros((EXT, 2 * PACKED), np.float32)
-    turn = np.zeros((6 * HALF, 2 * HALF), np.float32)
+    turn = np.zeros((5 * HALF, 2 * HALF), np.float32)
     for m in range(TRACE):
         for c in range(6):
+            for part in range(2):
+                place = part * PACKED + (c // 3) * TRIPLE + (c % 3) * TRACE + m
+                pad[c * PADDED + m, place] = 1
+        for c in range(3):
             for f in range(4):
-                pick[f * PACKED + c * TRACE + m, c * NODES + face_nodes[f, m]] = 1
-            for part in range(2):
-                pad[c * PADDED + m, part * PACKED + c * TRACE + m] = 1
-        for c in range(3):
-            for p in range(6):
+                pick[f * TRIPLE + c * TRACE + m, c * NODES + face_nodes[f, m]] = 1
+            for p in range(1, 6):
                 for part in range(2):
-                    turn[p * HALF + c * PADDED + m, part * HALF + c * PADDED + permuted[p, m]] = 1
+                    row = (p - 1) * HALF + c * PADDED
+                    turn[row + m, part * HALF + c * PADDED + permuted[p, m]] = 1
+    both = np.zeros((2 * EXT, 2 * PACKED), np.float32)
+    both[:EXT, :PACKED] = both[EXT:, PACKED:] = pad[:, :PACKED]
     spread_lift = np.zeros((2, 4 * TRACE, 8 * PADDED), np.float32)
     for f in range(4):
         for m in range(TRACE):
@@ -80,7 +85,7 @@
     spread_node = np.zeros((2, NODES, 2 * NODES), np.float32)
     spread_node[0, :, :NODES] = spread_node[0, :, NODES:] = np.eye(NODES)
     spread_node[1, :, :NODES] = np.eye(NODES)
-    return [a.astype(ml_dtypes.bfloat16) for a in (pick, pad, turn, spread_lift, spread_node)]
+    return [a.astype(ml_dtypes.bfloat16) for a in (pick, pad, both, turn, spread_lift, spread_node)]
 
 
 def mm(a, b):
@@ -109,14 +114,17 @@
 
 
 def traces_of(state, pick):
-    high, low = halves(state)
     parts = []
-    for part in (high, low):
-        all_faces = mm(pick, part).astype(BF16)
+    for half in range(2):
+        high, low = halves(state[half * 3 * NODES : (half + 1) * 3 * NODES])
+        faces = [mm(pick, part).astype(BF16) for part in (high, low)]
         parts.append(
-            jnp.concatenate([all_faces[f * PACKED : (f + 1) * PACKED] for f in range(4)], axis=1)
+            [
+                jnp.concatenate([x[f * TRIPLE : (f + 1) * TRIPLE] for f in range(4)], axis=1)
+                for x in faces
+            ]
         )
-    return jnp.concatenate(parts, axis=0)
+    return jnp.concatenate([parts[0][0], parts[1][0], parts[0][1], parts[1][1]], axis=0)
 
 
 def even_group():
@@ -166,9 +174,9 @@
 
 def turned(flux, permutation, turn):
     variants = mm(turn, stacked_values(flux))
-    out = variants[:HALF]
+    out = flux
     for p in range(1, 6):
-        out = jnp.where(permutation == p, variants[p * HALF : (p + 1) * HALF], out)
+        out = jnp.where(permutation == p, variants[(p - 1) * HALF : p * HALF], out)
     return out
 
 
@@ -293,15 +301,15 @@
     return jnp.concatenate([high, low], axis=0)
 
 
-def received_flux(tables, choice, geom_ref, permutation_ref, pad_ref, turn_ref):
+def received_flux(tables, choice, geom_ref, permutation_ref, both_ref, turn_ref):
     columns = [high_over_low(table) for table in tables]
     n, half = normals(geom_ref)
-    gathered = mm(jnp.concatenate(columns, axis=1), choice).astype(BF16)
-    flux = flux_h(mm(pad_ref[...], gathered), n, half)
+    table = mm(both_ref[...], jnp.concatenate(columns, axis=1)).astype(BF16)
+    flux = flux_h(split_product(table, choice), n, half)
     return turned(flux, row_of_faces(permutation_ref), turn_ref[...]), n
 
 
-def split_kernel(live_ref, swapped_ref, first_ref, other_ref):
+def split_kernel(live_ref, swapped_ref, other_ref, first_ref):
     slots = first_ref.shape[1]
     first_ref[...] = swapped_ref[:, :slots]
     other_ref[...] = swapped_ref[:, 2 * slots :]
@@ -313,15 +321,15 @@
     state_ref,
     residual_ref,
     partial_ref,
+    other_ref,
     first_ref,
-    other_ref,
     source_ref,
     geom_ref,
     permutation_ref,
     ratio_ref,
     curved_ref,
     lift_ref,
-    pad_ref,
+    both_ref,
     turn_ref,
     spread_lift_ref,
     pick_ref,
@@ -330,7 +338,7 @@
 ):
     tables = [r[...].reshape(-1, PACKED) for r in (first_ref, other_ref)]
     choice = partner_choice(row_of_faces(source_ref), tables[0].shape[0])
-    flux, n = received_flux(tables, choice, geom_ref, permutation_ref, pad_ref, turn_ref)
+    flux, n = received_flux(tables, choice, geom_ref, permutation_ref, both_ref, turn_ref)
     lifted = lifted_from(flux, n, stacked_weights(lift_ref[...], spread_lift_ref))
     scaling = jnp.where(curved_ref[...] == 1, ratio_ref[...], 1.0)
     scaling = scaling * alive(live_ref, scaling.shape[1])
@@ -382,7 +390,7 @@
     face_permutation,
 ):
     elements = fields.shape[2]
-    pick, pad, turn, spread_lift, spread_node = (jnp.asarray(a) for a in constant_matrices())
+    pick, pad, both, turn, spread_lift, spread_node = (jnp.asarray(a) for a in constant_matrices())
     slots = send_list.shape[3]
     send = send_list.reshape(24, slots)
     curved_row = curved.reshape(1, elements)
@@ -409,11 +417,11 @@
     residual = current
     for step in range(2):
         swapped = lax.all_to_all(outgoing, "sub", split_axis=0, concat_axis=0, tiled=True)
-        first, other = call(
+        other, first = call(
             split_kernel, VMEM, 1, [shape((8, slots, PACKED), F32)] * 2, "split", 1_000_000
         )(live_count, swapped)
+        other = swapped_pairs(other, "dom", 1)
         first = swapped_pairs(first, "dom", 0)
-        other = swapped_pairs(other, "dom", 1)
         partial = call(local_kernel, VMEM, 13, whole, "local", 4_000_000_000)(
             live_count,
             current,
@@ -438,15 +446,15 @@
             current,
             residual,
             partial,
+            other,
             first,
-            other,
             face_source,
             face_geom,
             face_permutation,
             jacobian_ratio,
             curved_row,
             lift_matrix,
-            pad,
+            both,
             turn,
             spread_lift,
             pick,

time: 58.8 us -> 56.4 us (0.959)
  the two profiles are of different devices: /device:TPU:256 before, /device:TPU:384 now
where the time goes in v4:
time: 56.4 us; the launch traced here: 56.1 us
  blocking collectives  24.5 us (43%)
  starting transfers between devices  14 us (25%)
  Pallas kernels  10.8 us (19%)
  waiting for transfers between devices  5.12 us (9%)
  between operations  1.55 us (3%)
    all_to_all x2, blocking collectives, on_device(): lax.all_to_all(outgoing, 'sub', split_axis=0, concat_axis=0, tiled=True)  24.5 us
    ppermute x4, starting transfers between devices, swapped_pairs(): return lax.ppermute(array, axis, pairs)  14 us
    ppermute x4, waiting for transfers between devices, swapped_pairs(): return lax.ppermute(array, axis, pairs)  5.12 us
    pallas_call x2, Pallas kernels, on_device(): call(local_kernel, VMEM, 13, whole, 'local', 4000000000)  4.56 us
    pallas_call x2, Pallas kernels, on_device(): call(functools.partial(final_kernel, step), VMEM, 16, shapes, 'final', 30...  4.14 us
    pallas_call x1, Pallas kernels, on_device(): call(first_kernel, HBM, 3, [outgoing_shape, whole, traces_shape], 'first'...  2.11 us
  transfers between devices with their start and end apart: 4, of which 2 were waited for; matrix products, arithmetic and copies ran while one was open for 0% of the time, Pallas kernels for 8%

profile of v4, /device:TPU:384, one launch (start us, length us, event | category | flops | bytes accessed | tf_op | source)
XLA Modules:
  0.0 56.1 jit_solution(4831438584228260930)
XLA Ops:
  1.3 2.1 %first.1 = (f32[8,96,128]{2,1,0:T(8,128)S(1)}, f32[6,56,256]{2,1,0:T(8,128)S(1)}, bf16[256,1024]{1,0:T(8,128)(2,1)S(1)}) custom-call(s32[1]{0:T(128)S(6)} %copy.19.live_ref, f32[6,56,256]{2,1,0:T(8,128)} %fields_hbm.1, s32[24,32]{1,0:T(8,128)} %bitcast.2, bf16[256,168]{1,0:T(8,128)(2,1)} %constant.12.clone.pick_hbm.pick_ref), custom_call_target="tpu_custom_call" | custom-call | flops 1000000000 | bytes 4000000 | tf_op jit(solution)/shard_map/first/pallas_call | solution.py:402
  3.4 0.0 copy-start.12
  3.4 0.0 copy-start.13
  3.4 13.2 %all_to_all.10.swapped_ref = f32[8,96,128]{2,1,0:T(8,128)S(1)} all-to-all(f32[8,96,128]{2,1,0:T(8,128)S(1)} %get-tuple-element.15), channel_id=1, replica_groups=mesh['dom'=64,'sub'=8] {'sub'}, dimensions={0} | all-to-all | bytes 786432 | tf_op jit(solution)/shard_map/all_to_all | solution.py:419
  16.6 0.0 copy-start
  16.6 0.0 copy-start.2
  16.6 0.0 copy-start.3
  16.6 0.0 copy-start.4
  16.6 0.0 copy-start.7
  16.6 0.0 copy-start.9
  16.6 0.0 copy-start.14
  16.7 0.0 copy-start.6
  16.7 6.7 %collective-permute-start = (f32[8,32,128]{2,1,0:T(8,128)S(1)}, f32[8,32,128]{2,1,0:T(8,128)S(1)}, u32[]{:S(2)}, u32[]{:S(2)}) collective-permute-start(f32[8,32,128]{2,1,0:T(8,128)S(1)} %get-tuple-element.16), channel_id=1, source_target_pairs={{8,16},{16,8},{24,32},{32,24},{40,48},{48,40},{56,64},{64,56},{72,... | collective-permute-start | bytes 393224 | tf_op jit(solution)/shard_map/ppermute | solution.py:33
  23.4 1.9 %collective-permute-start.1 = (f32[8,32,128]{2,1,0:T(8,128)S(1)}, f32[8,32,128]{2,1,0:T(8,128)S(1)}, u32[]{:S(2)}, u32[]{:S(2)}) collective-permute-start(f32[8,32,128]{2,1,0:T(8,128)S(1)} %get-tuple-element.17), channel_id=1, source_target_pairs={{0,8},{8,0},{16,24},{24,16},{32,40},{40,32},{48,56},{56,48},{64,72... | collective-permute-start | bytes 393224 | tf_op jit(solution)/shard_map/ppermute | solution.py:33
  25.3 0.0 copy-done.12
  25.3 0.0 copy-done.13
  25.3 0.0 copy-done
  25.4 0.0 copy-done.2
  25.4 0.0 copy-done.3
  25.4 0.0 copy-done.4
  25.4 0.0 copy-done.7
  25.4 0.0 copy-done.9
  25.4 0.0 copy-done.14
  25.4 0.0 copy-done.6
  25.4 0.0 copy-start.1
  25.4 0.0 copy-start.5
  25.5 0.0 copy-start.10
  25.5 0.0 copy-start.11
  25.5 2.3 %local.2.partial_ref = f32[6,56,256]{2,1,0:T(8,128)S(1)} custom-call(s32[1]{0:T(128)S(6)} %copy.19.live_ref, f32[6,56,256]{2,1,0:T(8,128)S(1)} %get-tuple-element.13.state_ref.residual_ref, bf16[256,1024]{1,0:T(8,128)(2,1)S(1)} %get-tuple-element.14.traces_ref, f32[9,256]{1,0:T(8,128)S(1)} %copy-done.3, f32[4,4,256]{2,1,0:T(4,128)S(1)} %copy-done.4, ...), custom_call_target="tpu_custom_call" | custom-call | flops 4000000000 | bytes 4000000 | tf_op jit(solution)/shard_map/local/pallas_call | solution.py:425
  27.8 0.0 copy-start.8
  27.8 0.0 collective-permute-done.other_ref
  27.8 2.5 %collective-permute-done.1.first_ref = f32[8,32,128]{2,1,0:T(8,128)S(1)} collective-permute-done((f32[8,32,128]{2,1,0:T(8,128)S(1)}, f32[8,32,128]{2,1,0:T(8,128)S(1)}, u32[]{:S(2)}, u32[]{:S(2)}) %collective-permute-start.1) | collective-permute-done | bytes 131104 | tf_op jit(solution)/shard_map/ppermute | solution.py:33
  30.3 0.0 copy-done.1
  30.3 0.0 copy-done.5
  30.3 0.0 copy-done.10
  30.3 0.0 copy-done.11
  30.3 0.0 copy-done.8
  30.3 2.0 %final.2 = (f32[6,56,256]{2,1,0:T(8,128)S(1)}, f32[6,56,256]{2,1,0:T(8,128)S(1)}, f32[8,96,128]{2,1,0:T(8,128)S(1)}, bf16[256,1024]{1,0:T(8,128)(2,1)S(1)}) custom-call(s32[1]{0:T(128)S(6)} %copy.19.live_ref, f32[6,56,256]{2,1,0:T(8,128)S(1)} %get-tuple-element.13.state_ref.residual_ref, f32[6,56,256]{2,1,0:T(8,128)S(1)} %get-tuple-element.13.state_ref.residual_ref, ...), custom_call_target="tpu_custom_call" | custom-call | flops 3000000000 | bytes 4000000 | tf_op jit(solution)/shard_map/final/pallas_call | solution.py:442
  32.3 11.3 %all_to_all.11.swapped_ref = f32[8,96,128]{2,1,0:T(8,128)S(1)} all-to-all(f32[8,96,128]{2,1,0:T(8,128)S(1)} %get-tuple-element.21), channel_id=1, replica_groups=mesh['dom'=64,'sub'=8] {'sub'}, dimensions={0} | all-to-all | bytes 786432 | tf_op jit(solution)/shard_map/all_to_all | solution.py:419
  43.7 3.4 %collective-permute-start.2 = (f32[8,32,128]{2,1,0:T(8,128)S(1)}, f32[8,32,128]{2,1,0:T(8,128)S(1)}, u32[]{:S(2)}, u32[]{:S(2)}) collective-permute-start(f32[8,32,128]{2,1,0:T(8,128)S(1)} %get-tuple-element.22), channel_id=1, source_target_pairs={{8,16},{16,8},{24,32},{32,24},{40,48},{48,40},{56,64},{64,56},{72,... | collective-permute-start | bytes 393224 | tf_op jit(solution)/shard_map/ppermute | solution.py:33
  47.1 1.9 %collective-permute-start.3 = (f32[8,32,128]{2,1,0:T(8,128)S(1)}, f32[8,32,128]{2,1,0:T(8,128)S(1)}, u32[]{:S(2)}, u32[]{:S(2)}) collective-permute-start(f32[8,32,128]{2,1,0:T(8,128)S(1)} %get-tuple-element.23), channel_id=1, source_target_pairs={{0,8},{8,0},{16,24},{24,16},{32,40},{40,32},{48,56},{56,48},{64,72... | collective-permute-start | bytes 393224 | tf_op jit(solution)/shard_map/ppermute | solution.py:33
  49.0 2.3 %local.3.partial_ref = f32[6,56,256]{2,1,0:T(8,128)S(1)} custom-call(s32[1]{0:T(128)S(6)} %copy.19.live_ref, f32[6,56,256]{2,1,0:T(8,128)S(1)} %get-tuple-element.18.state_ref, bf16[256,1024]{1,0:T(8,128)(2,1)S(1)} %get-tuple-element.20.traces_ref, f32[9,256]{1,0:T(8,128)S(1)} %copy-done.3, f32[4,4,256]{2,1,0:T(4,128)S(1)} %copy-done.4, ...), custom_call_target="tpu_custom_call" | custom-call | flops 4000000000 | bytes 4000000 | tf_op jit(solution)/shard_map/local/pallas_call | solution.py:425
  51.3 2.6 %collective-permute-done.2.other_ref = f32[8,32,128]{2,1,0:T(8,128)S(1)} collective-permute-done((f32[8,32,128]{2,1,0:T(8,128)S(1)}, f32[8,32,128]{2,1,0:T(8,128)S(1)}, u32[]{:S(2)}, u32[]{:S(2)}) %collective-permute-start.2) | collective-permute-done | bytes 131104 | tf_op jit(solution)/shard_map/ppermute | solution.py:33
  53.9 0.0 collective-permute-done.3.first_ref
  54.0 2.1 %final.3 = (f32[6,56,256]{2,1,0:T(8,128)}, f32[6,56,256]{2,1,0:T(8,128)}) custom-call(s32[1]{0:T(128)S(6)} %copy.19.live_ref, f32[6,56,256]{2,1,0:T(8,128)S(1)} %get-tuple-element.18.state_ref, f32[6,56,256]{2,1,0:T(8,128)S(1)} %get-tuple-element.19.residual_ref, f32[6,56,256]{2,1,0:T(8,128)S(1)} %local.3.partial_ref, ...), custom_call_target="tpu_custom_call" | custom-call | flops 3000000000 | bytes 4000000 | tf_op jit(solution)/shard_map/final/pallas_call | solution.py:442
  (2 shorter events, 0.0 us)
Async XLA Ops:
  3.4 21.9 %copy-start.12 = (bf16[2,84,192]{2,1,0:T(8,128)(2,1)S(1)}, bf16[2,84,192]{2,1,0:T(8,128)(2,1)}, u32[]{:S(2)}) copy-start(bf16[2,84,192]{2,1,0:T(8,128)(2,1)} %constant.16.clone.spread_lift_ref) | copy-start | bytes 193540
  3.4 21.9 %copy-start.13 = (bf16[144,256]{1,0:T(8,128)(2,1)S(1)}, bf16[144,256]{1,0:T(8,128)(2,1)}, u32[]{:S(2)}) copy-start(bf16[144,256]{1,0:T(8,128)(2,1)} %constant.13.clone.pad_ref) | copy-start | bytes 221188
  16.6 8.8 %copy-start = (f32[3,56,56]{2,1,0:T(8,128)S(1)}, f32[3,56,56]{2,1,0:T(8,128)}, u32[]{:S(2)}) copy-start(f32[3,56,56]{2,1,0:T(8,128)} %derivatives_ref.3) | copy-start | bytes 112900
  16.6 8.8 %copy-start.2 = (f32[56,84]{1,0:T(8,128)S(1)}, f32[56,84]{1,0:T(8,128)}, u32[]{:S(2)}) copy-start(f32[56,84]{1,0:T(8,128)} %lift_ref.7) | copy-start | bytes 56452
  16.6 8.8 %copy-start.3 = (f32[9,256]{1,0:T(8,128)S(1)}, f32[9,256]{1,0:T(8,128)}, u32[]{:S(2)}) copy-start(f32[9,256]{1,0:T(8,128)} %metric_ref.3) | copy-start | bytes 27652
  16.6 8.8 %copy-start.4 = (f32[4,4,256]{2,1,0:T(4,128)S(1)}, f32[4,4,256]{2,1,0:T(4,128)}, u32[]{:S(2)}) copy-start(f32[4,4,256]{2,1,0:T(4,128)} %geom_ref.7) | copy-start | bytes 49156
  16.6 8.8 %copy-start.7 = (s32[4,256]{1,0:T(4,128)S(1)}, s32[4,256]{1,0:T(4,128)}, u32[]{:S(2)}) copy-start(s32[4,256]{1,0:T(4,128)} %permutation_ref.7) | copy-start | bytes 12292
  16.6 8.8 %copy-start.9 = (bf16[360,144]{1,0:T(8,128)(2,1)S(1)}, bf16[360,144]{1,0:T(8,128)(2,1)}, u32[]{:S(2)}) copy-start(bf16[360,144]{1,0:T(8,128)(2,1)} %constant.15.clone.turn_ref) | copy-start | bytes 311044
  16.6 8.8 %copy-start.14 = (bf16[2,56,112]{2,1,0:T(8,128)(2,1)S(1)}, bf16[2,56,112]{2,1,0:T(8,128)(2,1)}, u32[]{:S(2)}) copy-start(bf16[2,56,112]{2,1,0:T(8,128)(2,1)} %constant.17.clone.spread_node_ref) | copy-start | bytes 75268
  16.7 8.7 %copy-start.6 = (s32[4,256]{1,0:T(4,128)S(1)}, s32[4,256]{1,0:T(4,128)}, u32[]{:S(2)}) copy-start(s32[4,256]{1,0:T(4,128)} %source_ref.7) | copy-start | bytes 12292
  16.7 11.1 %collective-permute-start = (f32[8,32,128]{2,1,0:T(8,128)S(1)}, f32[8,32,128]{2,1,0:T(8,128)S(1)}, u32[]{:S(2)}, u32[]{:S(2)}) collective-permute-start(f32[8,32,128]{2,1,0:T(8,128)S(1)} %get-tuple-element.16), channel_id=1, source_target_pairs={{8,16},{16,8},{24,32},{32,24},{40,48},{48,40},{56,64},{64,56},{72,... | collective-permute-start | bytes 393224 | tf_op jit(solution)/shard_map/ppermute | solution.py:33
  23.4 6.9 %collective-permute-start.1 = (f32[8,32,128]{2,1,0:T(8,128)S(1)}, f32[8,32,128]{2,1,0:T(8,128)S(1)}, u32[]{:S(2)}, u32[]{:S(2)}) collective-permute-start(f32[8,32,128]{2,1,0:T(8,128)S(1)} %get-tuple-element.17), channel_id=1, source_target_pairs={{0,8},{8,0},{16,24},{24,16},{32,40},{40,32},{48,56},{56,48},{64,72... | collective-permute-start | bytes 393224 | tf_op jit(solution)/shard_map/ppermute | solution.py:33
  25.4 4.8 %copy-start.1 = (f32[56,256]{1,0:T(8,128)S(1)}, f32[56,256]{1,0:T(8,128)}, u32[]{:S(2)}) copy-start(f32[56,256]{1,0:T(8,128)} %ratio_ref.3) | copy-start | bytes 172036
  25.4 4.8 %copy-start.5 = (s32[1,3,8,32]{3,2,1,0:T(8,128)S(1)}, s32[1,3,8,32]{3,2,1,0:T(8,128)}, u32[]{:S(2)}) copy-start(s32[1,3,8,32]{3,2,1,0:T(8,128)} %param.25) | copy-start | bytes 9220
  25.5 4.8 %copy-start.10 = (bf16[288,256]{1,0:T(8,128)(2,1)S(1)}, bf16[288,256]{1,0:T(8,128)(2,1)}, u32[]{:S(2)}) copy-start(bf16[288,256]{1,0:T(8,128)(2,1)} %constant.14.clone.both_ref) | copy-start | bytes 442372
  25.5 4.8 %copy-start.11 = (bf16[256,168]{1,0:T(8,128)(2,1)S(1)}, bf16[256,168]{1,0:T(8,128)(2,1)}, u32[]{:S(2)}) copy-start(bf16[256,168]{1,0:T(8,128)(2,1)} %constant.12.clone.pick_hbm.pick_ref) | copy-start | bytes 258052
  27.8 2.5 %copy-start.8 = (s32[256]{0:T(256)S(1)}, s32[256]{0:T(256)}, u32[]{:S(2)}) copy-start(s32[256]{0:T(256)} %param.21) | copy-start | bytes 3076
  43.7 10.3 %collective-permute-start.2 = (f32[8,32,128]{2,1,0:T(8,128)S(1)}, f32[8,32,128]{2,1,0:T(8,128)S(1)}, u32[]{:S(2)}, u32[]{:S(2)}) collective-permute-start(f32[8,32,128]{2,1,0:T(8,128)S(1)} %get-tuple-element.22), channel_id=1, source_target_pairs={{8,16},{16,8},{24,32},{32,24},{40,48},{48,40},{56,64},{64,56},{72,... | collective-permute-start | bytes 393224 | tf_op jit(solution)/shard_map/ppermute | solution.py:33
  47.1 6.9 %collective-permute-start.3 = (f32[8,32,128]{2,1,0:T(8,128)S(1)}, f32[8,32,128]{2,1,0:T(8,128)S(1)}, u32[]{:S(2)}, u32[]{:S(2)}) collective-permute-start(f32[8,32,128]{2,1,0:T(8,128)S(1)} %get-tuple-element.23), channel_id=1, source_target_pairs={{0,8},{8,0},{16,24},{24,16},{32,40},{40,32},{48,56},{56,48},{64,72... | collective-permute-start | bytes 393224 | tf_op jit(solution)/shard_map/ppermute | solution.py:33

commit v5 on v4

--- a/solution.py
+++ b/solution.py
@@ -288,25 +288,23 @@
         out_ref[c] = rate[c]
 
 
-def partner_choice(source, slots):
-    even = even_group()
-    near = source.shape[1]
-    far = near + 2 * slots
-    bases = [jnp.where(even, near, far), jnp.where(even, far, near)]
-    return jnp.concatenate([one_hot(source, slots, base) for base in bases], axis=0)
+def partner_gather(table, is_first, source_ref, both_ref):
+    source = row_of_faces(source_ref)
+    count = table.shape[0]
+    near, far = source.shape[1], source.shape[1] + 2 * count
+    base = jnp.where(even_group() == is_first, near, far)
+    padded = mm(both_ref[...], high_over_low(table)).astype(BF16)
+    return split_product(padded, one_hot(source, count, base))
+
+
+def early_kernel(live_ref, other_ref, source_ref, both_ref, out_ref):
+    table = other_ref[...].reshape(-1, PACKED)
+    out_ref[...] = partner_gather(table, False, source_ref, both_ref)
 
 
 def high_over_low(table):
     high, low = halves(jnp.transpose(table, (1, 0)))
     return jnp.concatenate([high, low], axis=0)
-
-
-def received_flux(tables, choice, geom_ref, permutation_ref, both_ref, turn_ref):
-    columns = [high_over_low(table) for table in tables]
-    n, half = normals(geom_ref)
-    table = mm(both_ref[...], jnp.concatenate(columns, axis=1)).astype(BF16)
-    flux = flux_h(split_product(table, choice), n, half)
-    return turned(flux, row_of_faces(permutation_ref), turn_ref[...]), n
 
 
 def split_kernel(live_ref, swapped_ref, other_ref, first_ref):
@@ -321,7 +319,7 @@
     state_ref,
     residual_ref,
     partial_ref,
-    other_ref,
+    early_ref,
     first_ref,
     source_ref,
     geom_ref,
@@ -336,9 +334,11 @@
     send_ref,
     *out_refs,
 ):
-    tables = [r[...].reshape(-1, PACKED) for r in (first_ref, other_ref)]
-    choice = partner_choice(row_of_faces(source_ref), tables[0].shape[0])
-    flux, n = received_flux(tables, choice, geom_ref, permutation_ref, both_ref, turn_ref)
+    n, half = normals(geom_ref)
+    exterior = early_ref[...] + partner_gather(
+        first_ref[...].reshape(-1, PACKED), True, source_ref, both_ref
+    )
+    flux = turned(flux_h(exterior, n, half), row_of_faces(permutation_ref), turn_ref[...])
     lifted = lifted_from(flux, n, stacked_weights(lift_ref[...], spread_lift_ref))
     scaling = jnp.where(curved_ref[...] == 1, ratio_ref[...], 1.0)
     scaling = scaling * alive(live_ref, scaling.shape[1])
@@ -438,6 +438,9 @@
             spread_node,
             swapped,
         )
+        early = call(
+            early_kernel, VMEM, 3, shape((EXT, 4 * elements), F32), "early", 1_000_000_000
+        )(live_count, other, face_source, both)
         shapes = [whole, whole] + ([outgoing_shape, traces_shape] if step == 0 else [])
         current, residual, *rest = call(
             functools.partial(final_kernel, step), VMEM, 16, shapes, "final", 3_000_000_000
@@ -446,7 +449,7 @@
             current,
             residual,
             partial,
-            other,
+            early,
             first,
             face_source,
             face_geom,

time: 56.4 us -> 57.3 us (1.016)
  starting transfers between devices: 14 us -> 15.1 us
  waiting for transfers between devices: 5.12 us -> 4.05 us
  Pallas kernels: 10.8 us -> 11.6 us
    ppermute x4, starting transfers between devices: 14 us -> 15.1 us  [swapped_pairs(): return lax.ppermute(array, axis, pairs)]
    ppermute x4, waiting for transfers between devices: 5.12 us -> 4.05 us  [swapped_pairs(): return lax.ppermute(array, axis, pairs)]
    pallas_call x0 -> x2, Pallas kernels: none -> 1.04 us  [on_device(): call(early_kernel, VMEM, 3, shape((EXT, 4 * elements), F32), 'early', 100...]
  transfers between devices with their start and end apart: 4 -> 4, of which waited for: 2 -> 3; matrix products, arithmetic and copies ran while one was open for 0% -> 0% of each run, Pallas kernels for 8% -> 10%
where the time goes in v5:
time: 57.3 us; the launch traced here: 57 us
  blocking collectives  24.5 us (43%)
  starting transfers between devices  15.1 us (26%)
  Pallas kernels  11.6 us (20%)
  waiting for transfers between devices  4.05 us (7%)
  between operations  1.56 us (3%)
    all_to_all x2, blocking collectives, on_device(): lax.all_to_all(outgoing, 'sub', split_axis=0, concat_axis=0, tiled=True)  24.5 us
    ppermute x4, starting transfers between devices, swapped_pairs(): return lax.ppermute(array, axis, pairs)  15.1 us
    pallas_call x2, Pallas kernels, on_device(): call(local_kernel, VMEM, 13, whole, 'local', 4000000000)  4.57 us
    ppermute x4, waiting for transfers between devices, swapped_pairs(): return lax.ppermute(array, axis, pairs)  4.05 us
    pallas_call x2, Pallas kernels, on_device(): call(functools.partial(final_kernel, step), VMEM, 16, shapes, 'final', 30...  3.87 us
    pallas_call x1, Pallas kernels, on_device(): call(first_kernel, HBM, 3, [outgoing_shape, whole, traces_shape], 'first'...  2.11 us
  transfers between devices with their start and end apart: 4, of which 3 were waited for; matrix products, arithmetic and copies ran while one was open for 0% of the time, Pallas kernels for 10%

profile of v5, /device:TPU:384, one launch (start us, length us, event | category | flops | bytes accessed | tf_op | source)
XLA Modules:
  0.0 57.0 jit_solution(18348767293301037553)
XLA Ops:
  1.3 2.1 %first.1 = (f32[8,96,128]{2,1,0:T(8,128)S(1)}, f32[6,56,256]{2,1,0:T(8,128)S(1)}, bf16[256,1024]{1,0:T(8,128)(2,1)S(1)}) custom-call(s32[1]{0:T(128)S(6)} %copy.19.live_ref, f32[6,56,256]{2,1,0:T(8,128)} %fields_hbm.1, s32[24,32]{1,0:T(8,128)} %bitcast.2, bf16[256,168]{1,0:T(8,128)(2,1)} %constant.12.clone.pick_hbm.pick_ref), custom_call_target="tpu_custom_call" | custom-call | flops 1000000000 | bytes 4000000 | tf_op jit(solution)/shard_map/first/pallas_call | solution.py:402
  3.4 0.0 copy-start.12
  3.4 0.0 copy-start.13
  3.4 13.2 %all_to_all.10.swapped_ref = f32[8,96,128]{2,1,0:T(8,128)S(1)} all-to-all(f32[8,96,128]{2,1,0:T(8,128)S(1)} %get-tuple-element.15), channel_id=1, replica_groups=mesh['dom'=64,'sub'=8] {'sub'}, dimensions={0} | all-to-all | bytes 786432 | tf_op jit(solution)/shard_map/all_to_all | solution.py:419
  16.6 0.0 copy-start
  16.6 0.0 copy-start.2
  16.6 0.0 copy-start.3
  16.6 0.0 copy-start.4
  16.6 0.0 copy-start.7
  16.6 0.0 copy-start.9
  16.6 0.0 copy-start.14
  16.7 0.0 copy-start.6
  16.7 6.7 %collective-permute-start = (f32[8,32,128]{2,1,0:T(8,128)S(1)}, f32[8,32,128]{2,1,0:T(8,128)S(1)}, u32[]{:S(2)}, u32[]{:S(2)}) collective-permute-start(f32[8,32,128]{2,1,0:T(8,128)S(1)} %get-tuple-element.16), channel_id=1, source_target_pairs={{8,16},{16,8},{24,32},{32,24},{40,48},{48,40},{56,64},{64,56},{72,... | collective-permute-start | bytes 393224 | tf_op jit(solution)/shard_map/ppermute | solution.py:33
  23.4 1.9 %collective-permute-start.1 = (f32[8,32,128]{2,1,0:T(8,128)S(1)}, f32[8,32,128]{2,1,0:T(8,128)S(1)}, u32[]{:S(2)}, u32[]{:S(2)}) collective-permute-start(f32[8,32,128]{2,1,0:T(8,128)S(1)} %get-tuple-element.17), channel_id=1, source_target_pairs={{0,8},{8,0},{16,24},{24,16},{32,40},{40,32},{48,56},{56,48},{64,72... | collective-permute-start | bytes 393224 | tf_op jit(solution)/shard_map/ppermute | solution.py:33
  25.3 0.0 copy-done.12
  25.3 0.0 copy-done.13
  25.3 0.0 copy-done
  25.4 0.0 copy-done.2
  25.4 0.0 copy-done.3
  25.4 0.0 copy-done.4
  25.4 0.0 copy-done.7
  25.4 0.0 copy-done.9
  25.4 0.0 copy-done.14
  25.4 0.0 copy-done.6
  25.4 0.0 copy-start.10
  25.4 2.3 %local.2.partial_ref = f32[6,56,256]{2,1,0:T(8,128)S(1)} custom-call(s32[1]{0:T(128)S(6)} %copy.19.live_ref, f32[6,56,256]{2,1,0:T(8,128)S(1)} %get-tuple-element.13.state_ref.residual_ref, bf16[256,1024]{1,0:T(8,128)(2,1)S(1)} %get-tuple-element.14.traces_ref, f32[9,256]{1,0:T(8,128)S(1)} %copy-done.3, f32[4,4,256]{2,1,0:T(4,128)S(1)} %copy-done.4, ...), custom_call_target="tpu_custom_call" | custom-call | flops 4000000000 | bytes 4000000 | tf_op jit(solution)/shard_map/local/pallas_call | solution.py:425
  27.7 0.0 copy-start.1
  27.7 0.0 copy-start.5
  27.8 0.0 copy-start.11
  27.8 0.0 collective-permute-done.other_ref
  27.8 0.0 copy-done.10
  27.8 0.5 early.2.early_ref
  28.3 0.0 copy-start.8
  28.3 1.9 %collective-permute-done.1.first_ref = f32[8,32,128]{2,1,0:T(8,128)S(1)} collective-permute-done((f32[8,32,128]{2,1,0:T(8,128)S(1)}, f32[8,32,128]{2,1,0:T(8,128)S(1)}, u32[]{:S(2)}, u32[]{:S(2)}) %collective-permute-start.1) | collective-permute-done | bytes 131104 | tf_op jit(solution)/shard_map/ppermute | solution.py:33
  30.3 0.0 copy-done.1
  30.3 0.0 copy-done.5
  30.3 0.0 copy-done.11
  30.3 0.0 copy-done.8
  30.3 1.9 %final.2 = (f32[6,56,256]{2,1,0:T(8,128)S(1)}, f32[6,56,256]{2,1,0:T(8,128)S(1)}, f32[8,96,128]{2,1,0:T(8,128)S(1)}, bf16[256,1024]{1,0:T(8,128)(2,1)S(1)}) custom-call(s32[1]{0:T(128)S(6)} %copy.19.live_ref, f32[6,56,256]{2,1,0:T(8,128)S(1)} %get-tuple-element.13.state_ref.residual_ref, f32[6,56,256]{2,1,0:T(8,128)S(1)} %get-tuple-element.13.state_ref.residual_ref, ...), custom_call_target="tpu_custom_call" | custom-call | flops 3000000000 | bytes 4000000 | tf_op jit(solution)/shard_map/final/pallas_call | solution.py:445
  32.2 11.3 %all_to_all.11.swapped_ref = f32[8,96,128]{2,1,0:T(8,128)S(1)} all-to-all(f32[8,96,128]{2,1,0:T(8,128)S(1)} %get-tuple-element.21), channel_id=1, replica_groups=mesh['dom'=64,'sub'=8] {'sub'}, dimensions={0} | all-to-all | bytes 786432 | tf_op jit(solution)/shard_map/all_to_all | solution.py:419
  43.6 4.6 %collective-permute-start.2 = (f32[8,32,128]{2,1,0:T(8,128)S(1)}, f32[8,32,128]{2,1,0:T(8,128)S(1)}, u32[]{:S(2)}, u32[]{:S(2)}) collective-permute-start(f32[8,32,128]{2,1,0:T(8,128)S(1)} %get-tuple-element.22), channel_id=1, source_target_pairs={{8,16},{16,8},{24,32},{32,24},{40,48},{48,40},{56,64},{64,56},{72,... | collective-permute-start | bytes 393224 | tf_op jit(solution)/shard_map/ppermute | solution.py:33
  48.1 1.9 %collective-permute-start.3 = (f32[8,32,128]{2,1,0:T(8,128)S(1)}, f32[8,32,128]{2,1,0:T(8,128)S(1)}, u32[]{:S(2)}, u32[]{:S(2)}) collective-permute-start(f32[8,32,128]{2,1,0:T(8,128)S(1)} %get-tuple-element.23), channel_id=1, source_target_pairs={{0,8},{8,0},{16,24},{24,16},{32,40},{40,32},{48,56},{56,48},{64,72... | collective-permute-start | bytes 393224 | tf_op jit(solution)/shard_map/ppermute | solution.py:33
  50.1 2.3 %local.3.partial_ref = f32[6,56,256]{2,1,0:T(8,128)S(1)} custom-call(s32[1]{0:T(128)S(6)} %copy.19.live_ref, f32[6,56,256]{2,1,0:T(8,128)S(1)} %get-tuple-element.18.state_ref, bf16[256,1024]{1,0:T(8,128)(2,1)S(1)} %get-tuple-element.20.traces_ref, f32[9,256]{1,0:T(8,128)S(1)} %copy-done.3, f32[4,4,256]{2,1,0:T(4,128)S(1)} %copy-done.4, ...), custom_call_target="tpu_custom_call" | custom-call | flops 4000000000 | bytes 4000000 | tf_op jit(solution)/shard_map/local/pallas_call | solution.py:425
  52.4 1.5 %collective-permute-done.2.other_ref = f32[8,32,128]{2,1,0:T(8,128)S(1)} collective-permute-done((f32[8,32,128]{2,1,0:T(8,128)S(1)}, f32[8,32,128]{2,1,0:T(8,128)S(1)}, u32[]{:S(2)}, u32[]{:S(2)}) %collective-permute-start.2) | collective-permute-done | bytes 131104 | tf_op jit(solution)/shard_map/ppermute | solution.py:33
  53.8 0.5 early.3.early_ref
  54.3 0.7 %collective-permute-done.3.first_ref = f32[8,32,128]{2,1,0:T(8,128)S(1)} collective-permute-done((f32[8,32,128]{2,1,0:T(8,128)S(1)}, f32[8,32,128]{2,1,0:T(8,128)S(1)}, u32[]{:S(2)}, u32[]{:S(2)}) %collective-permute-start.3) | collective-permute-done | bytes 131104 | tf_op jit(solution)/shard_map/ppermute | solution.py:33
  55.0 2.0 %final.3 = (f32[6,56,256]{2,1,0:T(8,128)}, f32[6,56,256]{2,1,0:T(8,128)}) custom-call(s32[1]{0:T(128)S(6)} %copy.19.live_ref, f32[6,56,256]{2,1,0:T(8,128)S(1)} %get-tuple-element.18.state_ref, f32[6,56,256]{2,1,0:T(8,128)S(1)} %get-tuple-element.19.residual_ref, f32[6,56,256]{2,1,0:T(8,128)S(1)} %local.3.partial_ref, f32[144,1024]{1,0:T(8,128)S(1)} %early.3.early_ref, ...), custom_call_target="tpu_custom_call" | custom-call | flops 3000000000 | bytes 4000000 | tf_op jit(solution)/shard_map/final/pallas_call | solution.py:445
  (2 shorter events, 0.0 us)
Async XLA Ops:
  3.4 21.9 %copy-start.12 = (bf16[2,84,192]{2,1,0:T(8,128)(2,1)S(1)}, bf16[2,84,192]{2,1,0:T(8,128)(2,1)}, u32[]{:S(2)}) copy-start(bf16[2,84,192]{2,1,0:T(8,128)(2,1)} %constant.16.clone.spread_lift_ref) | copy-start | bytes 193540
  3.4 21.9 %copy-start.13 = (bf16[144,256]{1,0:T(8,128)(2,1)S(1)}, bf16[144,256]{1,0:T(8,128)(2,1)}, u32[]{:S(2)}) copy-start(bf16[144,256]{1,0:T(8,128)(2,1)} %constant.13.clone.pad_ref) | copy-start | bytes 221188
  16.6 8.8 %copy-start = (f32[3,56,56]{2,1,0:T(8,128)S(1)}, f32[3,56,56]{2,1,0:T(8,128)}, u32[]{:S(2)}) copy-start(f32[3,56,56]{2,1,0:T(8,128)} %derivatives_ref.3) | copy-start | bytes 112900
  16.6 8.8 %copy-start.2 = (f32[56,84]{1,0:T(8,128)S(1)}, f32[56,84]{1,0:T(8,128)}, u32[]{:S(2)}) copy-start(f32[56,84]{1,0:T(8,128)} %lift_ref.7) | copy-start | bytes 56452
  16.6 8.8 %copy-start.3 = (f32[9,256]{1,0:T(8,128)S(1)}, f32[9,256]{1,0:T(8,128)}, u32[]{:S(2)}) copy-start(f32[9,256]{1,0:T(8,128)} %metric_ref.3) | copy-start | bytes 27652
  16.6 8.8 %copy-start.4 = (f32[4,4,256]{2,1,0:T(4,128)S(1)}, f32[4,4,256]{2,1,0:T(4,128)}, u32[]{:S(2)}) copy-start(f32[4,4,256]{2,1,0:T(4,128)} %geom_ref.7) | copy-start | bytes 49156
  16.6 8.8 %copy-start.7 = (s32[4,256]{1,0:T(4,128)S(1)}, s32[4,256]{1,0:T(4,128)}, u32[]{:S(2)}) copy-start(s32[4,256]{1,0:T(4,128)} %permutation_ref.7) | copy-start | bytes 12292
  16.6 8.8 %copy-start.9 = (bf16[360,144]{1,0:T(8,128)(2,1)S(1)}, bf16[360,144]{1,0:T(8,128)(2,1)}, u32[]{:S(2)}) copy-start(bf16[360,144]{1,0:T(8,128)(2,1)} %constant.15.clone.turn_ref) | copy-start | bytes 311044
  16.6 8.8 %copy-start.14 = (bf16[2,56,112]{2,1,0:T(8,128)(2,1)S(1)}, bf16[2,56,112]{2,1,0:T(8,128)(2,1)}, u32[]{:S(2)}) copy-start(bf16[2,56,112]{2,1,0:T(8,128)(2,1)} %constant.17.clone.spread_node_ref) | copy-start | bytes 75268
  16.7 8.7 %copy-start.6 = (s32[4,256]{1,0:T(4,128)S(1)}, s32[4,256]{1,0:T(4,128)}, u32[]{:S(2)}) copy-start(s32[4,256]{1,0:T(4,128)} %source_ref.11) | copy-start | bytes 12292
  16.7 11.1 %collective-permute-start = (f32[8,32,128]{2,1,0:T(8,128)S(1)}, f32[8,32,128]{2,1,0:T(8,128)S(1)}, u32[]{:S(2)}, u32[]{:S(2)}) collective-permute-start(f32[8,32,128]{2,1,0:T(8,128)S(1)} %get-tuple-element.16), channel_id=1, source_target_pairs={{8,16},{16,8},{24,32},{32,24},{40,48},{48,40},{56,64},{64,56},{72,... | collective-permute-start | bytes 393224 | tf_op jit(solution)/shard_map/ppermute | solution.py:33
  23.4 6.9 %collective-permute-start.1 = (f32[8,32,128]{2,1,0:T(8,128)S(1)}, f32[8,32,128]{2,1,0:T(8,128)S(1)}, u32[]{:S(2)}, u32[]{:S(2)}) collective-permute-start(f32[8,32,128]{2,1,0:T(8,128)S(1)} %get-tuple-element.17), channel_id=1, source_target_pairs={{0,8},{8,0},{16,24},{24,16},{32,40},{40,32},{48,56},{56,48},{64,72... | collective-permute-start | bytes 393224 | tf_op jit(solution)/shard_map/ppermute | solution.py:33
  25.4 2.4 %copy-start.10 = (bf16[288,256]{1,0:T(8,128)(2,1)S(1)}, bf16[288,256]{1,0:T(8,128)(2,1)}, u32[]{:S(2)}) copy-start(bf16[288,256]{1,0:T(8,128)(2,1)} %constant.14.clone.both_ref) | copy-start | bytes 442372
  27.7 2.5 %copy-start.1 = (f32[56,256]{1,0:T(8,128)S(1)}, f32[56,256]{1,0:T(8,128)}, u32[]{:S(2)}) copy-start(f32[56,256]{1,0:T(8,128)} %ratio_ref.3) | copy-start | bytes 172036
  27.7 2.5 %copy-start.5 = (s32[1,3,8,32]{3,2,1,0:T(8,128)S(1)}, s32[1,3,8,32]{3,2,1,0:T(8,128)}, u32[]{:S(2)}) copy-start(s32[1,3,8,32]{3,2,1,0:T(8,128)} %param.25) | copy-start | bytes 9220
  27.8 2.5 %copy-start.11 = (bf16[256,168]{1,0:T(8,128)(2,1)S(1)}, bf16[256,168]{1,0:T(8,128)(2,1)}, u32[]{:S(2)}) copy-start(bf16[256,168]{1,0:T(8,128)(2,1)} %constant.12.clone.pick_hbm.pick_ref) | copy-start | bytes 258052
  28.3 2.0 %copy-start.8 = (s32[256]{0:T(256)S(1)}, s32[256]{0:T(256)}, u32[]{:S(2)}) copy-start(s32[256]{0:T(256)} %param.21) | copy-start | bytes 3076
  43.6 10.3 %collective-permute-start.2 = (f32[8,32,128]{2,1,0:T(8,128)S(1)}, f32[8,32,128]{2,1,0:T(8,128)S(1)}, u32[]{:S(2)}, u32[]{:S(2)}) collective-permute-start(f32[8,32,128]{2,1,0:T(8,128)S(1)} %get-tuple-element.22), channel_id=1, source_target_pairs={{8,16},{16,8},{24,32},{32,24},{40,48},{48,40},{56,64},{64,56},{72,... | collective-permute-start | bytes 393224 | tf_op jit(solution)/shard_map/ppermute | solution.py:33
  48.1 6.9 %collective-permute-start.3 = (f32[8,32,128]{2,1,0:T(8,128)S(1)}, f32[8,32,128]{2,1,0:T(8,128)S(1)}, u32[]{:S(2)}, u32[]{:S(2)}) collective-permute-start(f32[8,32,128]{2,1,0:T(8,128)S(1)} %get-tuple-element.23), channel_id=1, source_target_pairs={{0,8},{8,0},{16,24},{24,16},{32,40},{40,32},{48,56},{56,48},{64,72... | collective-permute-start | bytes 393224 | tf_op jit(solution)/shard_map/ppermute | solution.py:33
